TPU v7x, 128 devices: a whole 4x4x4 slice. The times are simulated.
128 devices in a mesh: freq: 8 (over y, z_lo), rows: 16 (over z_hi, x, core).
Axes of the slice: x: 4, y: 4, z: 4 (z_hi: 2, z_lo: 2; z = z_hi * 2 + z_lo), core: 2. Of those that a mesh axis runs over, the one named last changes fastest.
Arguments:
- refl: bfloat16 [2, 16, 4608, 4608], P(None, 'freq', 'rows'), may hold values from -0.125 to 0.125
- refl_scale: float32 [16, 4608, 36], P('freq', 'rows'), may hold values from 0.5 to 4
- focus: bfloat16 [16, 4608, 128], P('freq', 'rows'), may hold values from -6 to 6
- first_mute: int32 [4608, 64], P('rows'), may hold values from 128 to 1023
- second_mute: int32 [64, 4608], P('freq', 'rows'), may hold values from 256 to 1023
Outputs:
- focus_next: float32 [64, 4608, 1024], P('freq', 'rows')
All inputs are finite; a program needn't handle non-finite values.
Results may differ from a plain program's by a relative error of at most 0.0085.
Values may be sent and summed in bfloat16 or wider, within the bound.
No kernel may reach another device: no remote copies, remote signals or barrier semaphores. Data moves between devices by JAX's collectives and lax.ppermute only.
A program may use at most 128 MiB of HBM per device.

v0:
```python
import math

import jax
import jax.numpy as jnp
from jax import lax
from jax.sharding import PartitionSpec as P

NT = 1024
LOWBIN = 24


def tables(freq_total):
    time_index = jnp.arange(NT, dtype=jnp.int32)
    freq_bins = LOWBIN + jnp.arange(freq_total, dtype=jnp.int32)
    phases = (freq_bins[:, None] * time_index[None, :] % NT).astype(jnp.float32) * (
        2.0 * math.pi / NT
    )
    inward = 1.0 / math.sqrt(2.0 * freq_total)
    outward = 2.0 / (NT * inward)
    basis_rows = jnp.concatenate([jnp.cos(phases), -jnp.sin(phases)], 0)
    return (basis_rows.T * inward, basis_rows * outward)


def split_basis(basis):
    upper = basis.astype(jnp.bfloat16)
    lower = (basis - upper.astype(jnp.float32)).astype(jnp.bfloat16)
    return (upper, lower)


def decode(quantized, block_scale):
    blocks = block_scale.shape[-1]
    reshaped = quantized.reshape(quantized.shape[:3] + (blocks, quantized.shape[3] // blocks))
    return (
        (reshaped * block_scale[None, :, :, :, None]).astype(jnp.bfloat16).reshape(quantized.shape)
    )


def combine_first(direct, crossed, points):
    return jnp.concatenate(
        [
            direct[..., :points] - crossed[..., points:],
            direct[..., points:] + crossed[..., :points],
        ],
        -1,
    )


def combine_second(direct, crossed, points):
    return jnp.concatenate(
        [
            direct[..., :points] + crossed[..., points:],
            direct[..., points:] - crossed[..., :points],
        ],
        -1,
    )


def mute_pass(samples, cutoff, inverse, forward):
    upper, lower = split_basis(inverse)
    traces = jnp.dot(upper, samples, preferred_element_type=jnp.float32) + jnp.dot(
        lower, samples, preferred_element_type=jnp.float32
    )
    time_index = jnp.arange(NT, dtype=jnp.int32)
    kept = jnp.where(time_index[:, None] < cutoff[None, :], traces, 0.0)
    return jnp.dot(forward, kept, precision=lax.Precision.HIGHEST).astype(jnp.bfloat16)


def on_device(refl, refl_scale, focus, first_mute, second_mute):
    groups = lax.axis_size("freq")
    freq_dev = refl.shape[1]
    rows_dev = refl.shape[2]
    points = focus.shape[2] // 2
    freq_total = freq_dev * groups
    inverse, forward = tables(freq_total)
    decoded = decode(refl, refl_scale)
    columns = decoded
    paired = jnp.einsum(
        "kfsn,fnc->kfsc",
        columns,
        lax.all_gather(focus, "rows", axis=1, tiled=True),
        preferred_element_type=jnp.float32,
    )
    focused = combine_first(paired[0], paired[1], points).astype(jnp.bfloat16)
    self_index = lax.axis_index("freq")
    block_size = points // groups
    exchanged = lax.all_to_all(
        focused.reshape(freq_dev, rows_dev, 2, points),
        "freq",
        split_axis=3,
        concat_axis=0,
        tiled=True,
    )
    samples = exchanged.transpose(2, 0, 1, 3).reshape(2 * freq_total, rows_dev * block_size)
    cutoff = lax.dynamic_slice_in_dim(first_mute, self_index * block_size, block_size, 1).reshape(
        rows_dev * block_size
    )
    spectra = mute_pass(samples, cutoff, inverse, forward)
    spectra = spectra.reshape(2, freq_total, rows_dev, block_size).transpose(1, 2, 0, 3)
    returned = lax.all_to_all(spectra, "freq", split_axis=0, concat_axis=3, tiled=True).reshape(
        freq_dev, rows_dev, 2 * points
    )
    point_share = points // groups
    columns = decoded
    products = jnp.einsum("kfsn,fsc->knfc", columns, returned, preferred_element_type=jnp.float32)
    summed = lax.psum_scatter(
        combine_second(products[0], products[1], points), "rows", scatter_dimension=0, tiled=True
    )
    adjoint_half = summed.astype(jnp.bfloat16).reshape(rows_dev, freq_dev, 2, points)
    regrouped = lax.all_to_all(adjoint_half, "freq", split_axis=3, concat_axis=1, tiled=True)
    final_samples = regrouped.transpose(3, 0, 2, 1).reshape(point_share * rows_dev, 2 * freq_total)
    upper, lower = split_basis(inverse.T)
    traces = jnp.dot(final_samples, upper, preferred_element_type=jnp.float32) + jnp.dot(
        final_samples, lower, preferred_element_type=jnp.float32
    )
    traces = traces.reshape(point_share, rows_dev, NT)
    time_index = jnp.arange(NT, dtype=jnp.int32)
    return jnp.where(time_index[None, None, :] < second_mute[:, :, None], traces, 0.0)


def solution(mesh):
    in_specs = (
        P(None, "freq", "rows", None),
        P("freq", "rows", None),
        P("freq", "rows", None),
        P("rows", None),
        P("freq", "rows"),
    )
    out_specs = P("freq", "rows", None)
    return jax.shard_map(
        on_device, mesh=mesh, in_specs=in_specs, out_specs=out_specs, check_vma=False
    )
```

profile of v0, /device:TPU:0, one launch (start us, length us, event | category | flops | bytes accessed | tf_op | source)
XLA Modules:
  0.0 245.4 jit_solution(14717921745920987155)
XLA Ops:
  6.5 0.0 copy-start
  6.5 0.0 all-gather.2.cloned.1.call-start
  6.5 0.7 all-gather.2.cloned.1.call-update
  7.3 1.0 copy.60
  8.3 6.3 %mul.70 = f32[2,288,36,128]{3,2,1,0:T(8,128)} broadcast(f32[2,288,36]{2,1,0:T(8,128)S(1)} %copy.60), dimensions={0,1,2} | broadcast | bytes 10699776 | tf_op jit(solution)/shard_map/mul | solution.py:34
  14.6 12.4 %mul.71 = f32[2,288,4608]{2,1,0:T(8,128)} reshape(f32[2,288,36,128]{3,2,1,0:T(8,128)} %mul.70) | data formatting | bytes 21233664 | tf_op jit(solution)/shard_map/mul | solution.py:34
  27.0 0.0 copy-done
  27.0 0.1 copy.59
  27.1 0.1 lt.45
  27.2 34.3 %all-gather.2.cloned.1.call-done = bf16[2,4608,128]{2,1,0:T(8,128)(2,1)} async-done(((bf16[2,288,128]{2,1,0:T(8,128)(2,1)}), bf16[2,4608,128]{2,1,0:T(8,128)(2,1)}) %all-gather.2.cloned.1.call-update) | async-done | bytes 2359312 | tf_op jit(solution)/shard_map/all_gather | solution.py:80
  61.5 9.3 %fusion.17 = f32[2,2,288,128]{3,2,0,1:T(8,128)S(1)} fusion(bf16[2,4608,128]{2,1,0:T(8,128)(2,1)} %all-gather.2.cloned.1.call-done, bf16[2,2,288,4608]{3,2,1,0:T(8,128)(2,1)} %param.5, f32[2,288,4608]{2,1,0:T(8,128)} %mul.71), kind=kOutput, calls=%fused_computation.22 | convolution fusion | flops 1374879744 | bytes 24182784 | tf_op jit(solution)/shard_map/kfsn,fnc->kfsc/dot_general | solution.py:77
  70.9 0.2 fusion.24
  71.1 0.1 pad_maximum_fusion.1
  71.2 0.9 copy.63
  72.1 4.4 %all-to-all-start = ((bf16[2,288,2,64]{1,2,0,3:T(2,128)(2,1)}), bf16[2,288,2,64]{1,2,0,3:T(2,128)(2,1)S(1)}, u32[]{:S(2)}, u32[]{:S(2)}) async-start(bf16[2,288,2,64]{1,2,0,3:T(2,128)(2,1)} %copy.63), calls=%async_computation | async-start | bytes 393216 | tf_op jit(solution)/shard_map/all_to_all | solution.py:86
  76.4 0.3 fusion.45
  76.8 6.6 %all-to-all-done = bf16[2,288,2,64]{1,2,0,3:T(2,128)(2,1)S(1)} async-done(((bf16[2,288,2,64]{1,2,0,3:T(2,128)(2,1)}), bf16[2,288,2,64]{1,2,0,3:T(2,128)(2,1)S(1)}, u32[]{:S(2)}, u32[]{:S(2)}) %all-to-all-start) | async-done | bytes 147488 | tf_op jit(solution)/shard_map/all_to_all | solution.py:86
  83.4 1.6 copy.66
  85.1 0.5 reshape.34
  85.6 1.4 fusion.32
  87.1 1.4 fusion.44
  88.5 0.0 copy-start.3
  88.5 6.4 %fusion.13 = bf16[32,2304]{1,0:T(8,128)(2,1)S(1)} fusion(f32[1024,2304]{1,0:T(8,128)S(1)} %fusion.44, f32[1024,2304]{1,0:T(8,128)S(1)} %fusion.32, s32[2304]{0:T(1024)S(1)} %lt.45, f32[16,1024]{1,0:T(8,128)S(1)} %get-tuple-element.14, f32[16,1024]{1,0:T(8,128)S(1)} %get-tuple-element.13), kind=kOutput, calls=%fused_computation.18 | convolution fusion | flops 913186816 | bytes 19162112 | tf_op jit(solution)/shard_map/dot_general | solution.py:65
  94.9 0.3 copy.67
  95.3 0.5 reshape.35
  95.7 2.3 copy.68
  98.0 3.6 %all-to-all-start.1 = ((bf16[16,288,2,8]{1,3,2,0:T(8,128)(2,1)}), bf16[16,288,2,8]{1,3,2,0:T(8,128)(2,1)S(1)}, u32[]{:S(2)}, u32[]{:S(2)}) async-start(bf16[16,288,2,8]{1,3,2,0:T(8,128)(2,1)} %copy.68), calls=%async_computation.1 | async-start | bytes 393216 | tf_op jit(solution)/shard_map/all_to_all | solution.py:99
  101.6 0.0 copy-done.3
  101.6 0.6 dynamic-slice
  102.8 5.2 %all-to-all-done.1 = bf16[16,288,2,8]{1,3,2,0:T(8,128)(2,1)S(1)} async-done(((bf16[16,288,2,8]{1,3,2,0:T(8,128)(2,1)}), bf16[16,288,2,8]{1,3,2,0:T(8,128)(2,1)S(1)}, u32[]{:S(2)}, u32[]{:S(2)}) %all-to-all-start.1) | async-done | bytes 147488 | tf_op jit(solution)/shard_map/all_to_all | solution.py:99
  108.0 8.6 %fusion.8 = f32[2,4608,2,128]{1,3,0,2:T(8,128)S(1)} fusion(bf16[2,288,128,1]{1,2,3,0:T(8,128)(2,1)S(1)} %bitcast.80, bf16[2,2,288,4608]{3,2,1,0:T(8,128)(2,1)} %param.5, f32[2,288,4608]{2,1,0:T(8,128)} %mul.71), kind=kOutput, calls=%fused_computation.11 | convolution fusion | flops 1374879744 | bytes 30818304 | tf_op jit(solution)/shard_map/kfsn,fsc->knfc/dot_general | solution.py:104
  116.6 0.6 slice_bitcast_fusion.1
  117.3 0.5 slice_add_fusion
  117.8 2.5 %pad_maximum_fusion = f32[4608,2,128]{0,2,1:T(8,128)} fusion(f32[4608,2,64]{0,2,1:T(8,128)S(1)} %get-tuple-element.6, f32[4608,2,64]{0,2,1:T(8,128)S(1)} %get-tuple-element.5), kind=kLoop, calls=%fused_computation.15 | loop fusion | flops 1179648 | bytes 9437184 | tf_op jit(solution)/shard_map/concatenate | solution.py:49
  120.3 8.0 %copy.73 = f32[4608,2,128]{2,1,0:T(2,128)} copy(f32[4608,2,128]{0,2,1:T(8,128)} %pad_maximum_fusion) | data formatting | bytes 9437184 | tf_op jit(solution)/shard_map/concatenate | solution.py:49
  128.4 93.2 %all-reduce.2 = bf16[4608,2,128]{2,1,0:T(2,128)(2,1)S(1)} all-reduce(f32[4608,2,128]{2,1,0:T(2,128)} %copy.73), channel_id=2, replica_groups=mesh['freq'=8,'rows'=16] {'rows'}, use_global_device_ids=true, to_apply=%region_0.1.clone | all-reduce | flops 1179648 | bytes 7077888
  221.6 0.1 constant_dynamic-slice_fusion
  221.7 0.2 copy.74
  221.9 0.2 copy.75
  222.1 9.2 %all_to_all.51 = bf16[288,2,2,64]{0,2,1,3:T(2,128)(2,1)S(1)} all-to-all(bf16[288,2,2,64]{0,2,1,3:T(2,128)(2,1)S(1)} %copy.75), channel_id=1, replica_groups=mesh['freq'=8,'rows'=16] {'freq'}, dimensions={3} | all-to-all | bytes 294912 | tf_op jit(solution)/shard_map/all_to_all | solution.py:109
  231.4 0.2 reshape.38
  231.5 1.4 fusion.42
  232.9 0.0 copy-start.2
  233.0 1.4 convolution_add_fusion
  234.4 0.0 copy-start.1
  234.4 0.0 copy-done.2
  234.4 4.2 %fusion.3 = f32[8,288,1024]{2,1,0:T(8,128)} fusion(f32[8,288,1024]{2,1,0:T(8,128)S(1)} %bitcast.78, s32[8,288]{1,0:T(8,128)S(1)} %copy-done.2), kind=kLoop, calls=%fused_computation.6 | loop fusion | flops 4718592 | bytes 18883584 | tf_op jit(solution)/shard_map/jit(_where)/select_n | solution.py:117
  238.6 0.0 copy-done.1
  (9 shorter events, 0.2 us)
Async XLA Ops:
  6.5 20.4 %copy-start = (s32[288,64]{0,1:T(8,128)S(1)}, s32[288,64]{0,1:T(8,128)}, u32[]{:S(2)}) copy-start(s32[288,64]{0,1:T(8,128)} %param.8) | copy-start | bytes 221188
  6.5 55.0 %all-gather.2.cloned.1.call-start = ((), (), s32[]{:S(2)}) async-start(), calls=%async_computation.3 | async-start | bytes 2506752 | tf_op jit(solution)/shard_map/all_gather | solution.py:80
  72.1 11.3 %all-to-all-start = ((bf16[2,288,2,64]{1,2,0,3:T(2,128)(2,1)}), bf16[2,288,2,64]{1,2,0,3:T(2,128)(2,1)S(1)}, u32[]{:S(2)}, u32[]{:S(2)}) async-start(bf16[2,288,2,64]{1,2,0,3:T(2,128)(2,1)} %copy.63), calls=%async_computation | async-start | bytes 393216 | tf_op jit(solution)/shard_map/all_to_all | solution.py:86
  88.5 13.1 %copy-start.3 = (u32[128]{0:T(128)S(1)}, u32[128]{0:T(128)}, u32[]{:S(2)}) copy-start(u32[128]{0:T(128)} %constant.41) | copy-start | bytes 1540
  98.0 10.0 %all-to-all-start.1 = ((bf16[16,288,2,8]{1,3,2,0:T(8,128)(2,1)}), bf16[16,288,2,8]{1,3,2,0:T(8,128)(2,1)S(1)}, u32[]{:S(2)}, u32[]{:S(2)}) async-start(bf16[16,288,2,8]{1,3,2,0:T(8,128)(2,1)} %copy.68), calls=%async_computation.1 | async-start | bytes 393216 | tf_op jit(solution)/shard_map/all_to_all | solution.py:99
  232.9 1.4 copy-start.2
  234.4 4.2 %copy-start.1 = (s32[288,64]{0,1:T(8,128)S(1)}, s32[288,64]{0,1:T(8,128)}, u32[]{:S(2)}) copy-start(s32[288,64]{0,1:T(8,128)} %param.8) | copy-start | bytes 221188
Sparse Core Ops, SparseCore 0:
  9.8 51.6 all-gather.1
where the time goes:
time: 246 us; the launch traced here: 245 us
  blocking collectives  102 us (41%)
  waiting for transfers between devices  46.8 us (19%)
  local copies, waits for them, and re-layouts  36.1 us (15%)
  matrix products  30.1 us (12%)
  between operations  14.2 us (6%)
  starting transfers between devices  7.99 us (3%)
  other arithmetic  7.83 us (3%)
    unnamed x1, blocking collectives  93.2 us
    all_gather x1, waiting for transfers between devices, on_device(): lax.all_gather(focus, 'rows', axis=1, tiled=True)  34.3 us
    mul x2, local copies, waits for them, and re-layouts, decode(): reshaped * block_scale[None, :, :, :, None]  18.7 us
    dot_general x1, matrix products, on_device(): jnp.einsum('kfsn,fnc->kfsc', columns, lax.all_gather(focus, 'rows', axis=...  9.34 us
    all_to_all x1, blocking collectives, on_device(): lax.all_to_all(adjoint_half, 'freq', split_axis=3, concat_axis=1, tiled=T...  9.18 us
    dot_general x1, matrix products, on_device(): jnp.einsum('kfsn,fsc->knfc', columns, returned, preferred_element_type=jn...  8.6 us
    concatenate x1, local copies, waits for them, and re-layouts, combine_second(): jnp.concatenate([direct[..., :points] + crossed[..., points:], direct[......  8.04 us
    all_to_all x1, waiting for transfers between devices, on_device(): lax.all_to_all(focused.reshape(freq_dev, rows_dev, 2, points), 'freq', sp...  6.59 us
  transfers between devices with their start and end apart: 3, of which 3 were waited for; matrix products, arithmetic and copies ran while one was open for 9% of the time, Pallas kernels for 0%

commit v1 on v0

v1 whole, which is shorter than its diff:
```python
import math

import jax
import jax.numpy as jnp
import numpy as np
from jax import lax
from jax.experimental import pallas as pl
from jax.experimental.pallas import tpu as pltpu
from jax.sharding import Mesh
from jax.sharding import PartitionSpec as P

NT = 1024
LOWBIN = 24
FREQ = ("y", "zl")
ROWS = ("zh", "x", "c")
SWAP = ((0, 1), (1, 0))
BF = jnp.bfloat16
F32 = jnp.float32
MB = 1 << 20


def tables(freq_total):
    phases = (
        (LOWBIN + np.arange(freq_total))[:, None] * np.arange(NT)[None, :] % NT
    ) * (2.0 * math.pi / NT)
    inward = 1.0 / math.sqrt(2.0 * freq_total)
    outward = 2.0 / (NT * inward)
    rows = np.stack([np.cos(phases), -np.sin(phases)], 1).reshape(2 * freq_total, NT)
    return rows * inward, rows * outward


def split(table):
    upper = table.astype(BF)
    lower = (table - upper.astype(np.float64)).astype(BF)
    return upper, lower


def constants(freq_total, group):
    inverse, forward = tables(freq_total)
    rows = 2 * freq_total
    upper, lower = split(inverse)
    pair = np.concatenate([upper, lower], 0)
    zero = np.zeros_like(pair)
    inv = np.stack([np.concatenate([pair, zero], 0), np.concatenate([zero, pair], 0)])
    spread = np.zeros((rows * group, 2 * rows * group), BF)
    for q in range(rows):
        for p in range(group):
            for h in range(2):
                spread[q * group + p, p * 2 * rows + h * rows + q] = 1
    fwd = np.zeros((NT, 128), BF)
    fwd[:, :rows] = forward.T.astype(BF)
    back = np.zeros((group, 128, rows * group), BF)
    for q in range(rows):
        for p in range(group):
            back[p, q, q * group + p] = 1
    return inv, spread, fwd, back


def decode_kernel(refl_ref, scale_ref, out_ref):
    blocks = scale_ref.shape[-1]
    for b in range(blocks):
        scale = scale_ref[0, :, b : b + 1]
        for k in range(2):
            part = refl_ref[k, 0, :, b * 128 : (b + 1) * 128].astype(F32)
            out_ref[k, 0, :, b * 128 : (b + 1) * 128] = (part * scale).astype(BF)


def decode(refl, scale):
    _, freqs, rows, cols = refl.shape
    step = 48
    return pl.pallas_call(
        decode_kernel,
        grid=(freqs, rows // step),
        in_specs=[
            pl.BlockSpec((2, 1, step, cols), lambda f, s: (0, f, s, 0)),
            pl.BlockSpec((1, step, scale.shape[-1]), lambda f, s: (f, s, 0)),
        ],
        out_specs=pl.BlockSpec((2, 1, step, cols), lambda f, s: (0, f, s, 0)),
        out_shape=jax.ShapeDtypeStruct(refl.shape, BF),
        compiler_params=pltpu.CompilerParams(vmem_limit_bytes=16 * MB),
        cost_estimate=pl.CostEstimate(
            flops=refl.size, bytes_accessed=4 * refl.size, transcendentals=0
        ),
        name="decode",
    )(refl, scale)


def first_kernel(pick_ref, dec_ref, focus_ref, *rest):
    out_ref, acc_ref = rest[-2], rest[-1]
    k = pl.program_id(0)
    rows = dec_ref.shape[2]
    part = jnp.dot(
        dec_ref[...].reshape(2 * rows, dec_ref.shape[3]),
        focus_ref[...],
        preferred_element_type=F32,
    )

    @pl.when(k == 0)
    def _():
        acc_ref[...] = part

    @pl.when(k > 0)
    def _():
        acc_ref[...] += part

    @pl.when(k == pl.num_programs(0) - 1)
    def _():
        direct = acc_ref[:rows]
        crossed = pltpu.roll(acc_ref[rows:], 64, 1)
        lane = lax.broadcasted_iota(jnp.int32, direct.shape, 1)
        both = direct + jnp.where(lane < 64, -crossed, crossed)
        turned = both.T.reshape(2, 8, 8, rows)
        out_ref[:, 0] = jnp.concatenate([turned[0], turned[1]], 1).astype(BF)


def first_product(pick, decoded, focus, partial):
    _, freqs, rows, cols = decoded.shape
    step = 1152
    extra = [] if partial is None else [partial]
    return pl.pallas_call(
        first_kernel,
        grid_spec=pltpu.PrefetchScalarGridSpec(
            num_scalar_prefetch=1,
            grid=(cols // step,),
            in_specs=[
                pl.BlockSpec((2, 1, rows, step), lambda k, pick: (0, pick[0], 0, k)),
                pl.BlockSpec((step, 128), lambda k, pick: (k, 0)),
            ]
            + [pl.BlockSpec(memory_space=pl.ANY) for _ in extra],
            out_specs=pl.BlockSpec((8, 1, 16, rows), lambda k, pick: (0, pick[0], 0, 0)),
            scratch_shapes=[pltpu.VMEM((2 * rows, 128), F32)],
        ),
        out_shape=jax.ShapeDtypeStruct((8, freqs, 16, rows), BF),
        input_output_aliases={3: 0} if extra else {},
        compiler_params=pltpu.CompilerParams(vmem_limit_bytes=16 * MB),
        cost_estimate=pl.CostEstimate(
            flops=4 * rows * cols * 128, bytes_accessed=4 * rows * cols, transcendentals=0
        ),
        name="first_product",
    )(pick, decoded, focus, *extra)


def pick_column(table, column):
    lane = lax.broadcasted_iota(jnp.int32, table.shape, 1)
    return jnp.sum(jnp.where(lane == column, table, 0.0), 1, keepdims=True)


def mute_kernel(group_ref, in_ref, cut_ref, spread_ref, inv_ref, fwd_ref, back_ref, out_ref, wide_ref, ret_ref):
    p = pl.program_id(0)
    rows = in_ref.shape[-1]

    @pl.when(p == 0)
    def _():
        turned = in_ref[...].reshape(256, rows).astype(F32).T.astype(BF)
        wide = jnp.dot(turned, spread_ref[...], preferred_element_type=F32)
        for q in range(4):
            wide_ref[q] = wide[:, q * 128 : (q + 1) * 128].astype(BF)

    traces = jnp.dot(wide_ref[p // 2], inv_ref[p % 2], preferred_element_type=F32)
    cut = pick_column(cut_ref[...].astype(F32), group_ref[0] * 8 + p).astype(jnp.int32)
    time = lax.broadcasted_iota(jnp.int32, traces.shape, 1)
    kept = jnp.where(time < cut, traces, 0.0).astype(BF)
    ret_ref[p] = jnp.dot(kept, fwd_ref[...], preferred_element_type=F32).astype(BF)

    @pl.when(p == pl.num_programs(0) - 1)
    def _():
        total = jnp.dot(ret_ref[0], back_ref[0], preferred_element_type=F32)
        for q in range(1, 8):
            total += jnp.dot(ret_ref[q], back_ref[q], preferred_element_type=F32)
        out_ref[...] = total.T.reshape(8, 2, 16, rows).astype(BF)


def whole(array):
    zeros = (0,) * array.ndim
    return pl.BlockSpec(array.shape, lambda *_: zeros)


def mute(group, samples, cut, spread, inv, fwd, back):
    rows = samples.shape[-1]
    args = (samples, cut, spread, inv, fwd, back)
    return pl.pallas_call(
        mute_kernel,
        grid_spec=pltpu.PrefetchScalarGridSpec(
            num_scalar_prefetch=1,
            grid=(8,),
            in_specs=[whole(a) for a in args],
            out_specs=pl.BlockSpec(samples.shape, lambda *_: (0, 0, 0, 0)),
            scratch_shapes=[pltpu.VMEM((4, rows, 128), BF), pltpu.VMEM((8, rows, 128), BF)],
        ),
        out_shape=jax.ShapeDtypeStruct(samples.shape, BF),
        compiler_params=pltpu.CompilerParams(vmem_limit_bytes=24 * MB),
        cost_estimate=pl.CostEstimate(
            flops=8 * rows * NT * 512, bytes_accessed=4 * MB, transcendentals=0
        ),
        name="mute",
    )(group, *args)


def second_kernel(core_ref, ret_ref, dec_ref, keep_ref, send_ref, lhs_ref):
    rows = dec_ref.shape[2]

    @pl.when(pl.program_id(1) == 0)
    def _():
        direct = ret_ref[...].reshape(8, 16, rows).astype(F32)
        crossed = jnp.concatenate([direct[:, 8:], -direct[:, :8]], 1)
        lhs_ref[...] = jnp.concatenate(
            [direct.reshape(128, rows), crossed.reshape(128, rows)], 1
        ).astype(BF)

    out = jnp.dot(
        lhs_ref[...],
        dec_ref[...].reshape(2 * rows, dec_ref.shape[3]),
        preferred_element_type=F32,
    )
    even = core_ref[0] == 0
    for j in range(2):
        left = out[:, 2 * j * rows : (2 * j + 1) * rows].reshape(8, 16, rows)
        right = out[:, (2 * j + 1) * rows : (2 * j + 2) * rows].reshape(8, 16, rows)
        keep_ref[:, j, 0] = jnp.where(even, left, right).astype(BF)
        send_ref[:, j, 0] = jnp.where(even, right, left).astype(BF)


def second_product(core, returned, decoded):
    _, freqs, rows, cols = decoded.shape
    step = 4 * rows
    shape = jax.ShapeDtypeStruct((8, 8, freqs, 16, rows), BF)
    spec = pl.BlockSpec((8, 2, 1, 16, rows), lambda f, k, core: (0, k, f, 0, 0))
    return pl.pallas_call(
        second_kernel,
        grid_spec=pltpu.PrefetchScalarGridSpec(
            num_scalar_prefetch=1,
            grid=(freqs, cols // step),
            in_specs=[
                pl.BlockSpec((8, 1, 16, rows), lambda f, k, core: (0, f, 0, 0)),
                pl.BlockSpec((2, 1, rows, step), lambda f, k, core: (0, f, 0, k)),
            ],
            out_specs=[spec, spec],
            scratch_shapes=[pltpu.VMEM((128, 2 * rows), BF)],
        ),
        out_shape=[shape, shape],
        compiler_params=pltpu.CompilerParams(vmem_limit_bytes=24 * MB),
        cost_estimate=pl.CostEstimate(
            flops=8 * rows * cols * 128, bytes_accessed=10 * rows * cols, transcendentals=0
        ),
        name="second_product",
    )(core, returned, decoded)


def final_kernel(in_ref, cut_ref, spread_ref, inv_ref, out_ref, wide_ref, edge_ref):
    p = pl.program_id(0)
    rows = in_ref.shape[-1]

    @pl.when(p == 0)
    def _():
        total = in_ref[:, 0].astype(F32)
        for j in range(1, 8):
            total += in_ref[:, j].astype(F32)
        turned = total.reshape(256, rows).T.astype(BF)
        wide = jnp.dot(turned, spread_ref[...], preferred_element_type=F32)
        for q in range(4):
            wide_ref[q] = wide[:, q * 128 : (q + 1) * 128].astype(BF)
        edge_ref[...] = cut_ref[...].astype(F32).T

    traces = jnp.dot(wide_ref[p // 2], inv_ref[p % 2], preferred_element_type=F32)
    cut = pick_column(edge_ref[...], p).astype(jnp.int32)
    time = lax.broadcasted_iota(jnp.int32, traces.shape, 1)
    out_ref[0] = jnp.where(time < cut, traces, 0.0)


def final(partials, cut, spread, inv):
    rows = partials.shape[-1]
    args = (partials, cut, spread, inv)
    return pl.pallas_call(
        final_kernel,
        grid=(8,),
        in_specs=[whole(a) for a in args],
        out_specs=pl.BlockSpec((1, rows, NT), lambda p: (p, 0, 0)),
        scratch_shapes=[pltpu.VMEM((4, rows, 128), BF), pltpu.VMEM((rows, 8), F32)],
        out_shape=jax.ShapeDtypeStruct((8, rows, NT), F32),
        compiler_params=pltpu.CompilerParams(vmem_limit_bytes=24 * MB),
        cost_estimate=pl.CostEstimate(
            flops=8 * rows * NT * 256, bytes_accessed=12 * MB, transcendentals=0
        ),
        name="final",
    )(*args)


def on_device(refl, refl_scale, focus, first_mute, second_mute):
    _, freqs, rows, _ = refl.shape
    core = lax.axis_index("c").astype(jnp.int32)[None]
    group = lax.axis_index(FREQ).astype(jnp.int32)[None]
    inv, spread, fwd, back = (jnp.asarray(a) for a in constants(8 * freqs, 8))

    shares = jnp.broadcast_to(focus[None], (8, 2, rows, 128)).reshape(16, rows, 128)
    own = lax.all_to_all(shares, ROWS, 0, 0, tiled=True).reshape(16 * rows, 128)
    decoded = decode(refl, refl_scale)
    other = lax.ppermute(own, "c", SWAP)
    half = first_product(core, decoded, own, None)
    focused = first_product(1 - core, decoded, other, half)
    samples = lax.all_to_all(focused, FREQ, 0, 0, tiled=True)
    spectra = mute(group, samples, first_mute, spread, inv, fwd, back)
    returned = lax.all_to_all(spectra, FREQ, 0, 0, tiled=True)
    keep, send = second_product(core, returned, decoded)
    got = lax.ppermute(send, "c", SWAP)
    summed = (keep.astype(F32) + got.astype(F32)).astype(BF)
    partials = lax.all_to_all(
        summed.reshape(64, 2 * 16, rows), FREQ + ("zh", "x"), 0, 0, tiled=True
    )
    return final(partials.reshape(8, 8, 32, rows), second_mute, spread, inv)


def solution(mesh):
    fine = Mesh(mesh.devices.reshape(4, 2, 2, 4, 2), ("y", "zl", "zh", "x", "c"))
    in_specs = (
        P(None, FREQ, ROWS, None),
        P(FREQ, ROWS, None),
        P(FREQ, ROWS, None),
        P(ROWS, None),
        P(FREQ, ROWS),
    )
    return jax.shard_map(
        on_device, mesh=fine, in_specs=in_specs, out_specs=P(FREQ, ROWS, None), check_vma=False
    )
```

time: 246 us -> 123 us (0.50)
  waiting for transfers between devices: 46.8 us -> 10.2 us
  blocking collectives: 102 us -> 65.8 us
  Pallas kernels: 0 us -> 31.9 us
  matrix products: 30.1 us -> 0 us
  local copies, waits for them, and re-layouts: 36.1 us -> 9.42 us
  between operations: 14.2 us -> 0.14 us
  other arithmetic: 7.83 us -> 0.45 us
  starting transfers between devices: 7.99 us -> 5.13 us
    unnamed x1 -> x0, blocking collectives: 93.2 us -> none
    all_to_all x1 -> x3, blocking collectives: 9.18 us -> 65.8 us  [the longest x1 29.7 us: on_device(): lax.all_to_all(summed.reshape(64, 2 * 16, rows), FREQ + ('zh', 'x'), 0, 0...]
    all_gather x1 -> x0, waiting for transfers between devices: 34.3 us -> none  [on_device(): lax.all_gather(focus, 'rows', axis=1, tiled=True)]
    pallas_call x0 -> x6, Pallas kernels: none -> 31.9 us  [the longest x2 7.64 us: first_product(): pl.pallas_call(first_kernel, grid_spec=pltpu.PrefetchScalarGridSpec(num_s...]
    dot_general x7 -> x0, matrix products: 30.1 us -> none  [the longest x1 9.34 us: on_device(): jnp.einsum('kfsn,fnc->kfsc', columns, lax.all_gather(focus, 'rows', axis=...]
    mul x2 -> x0, local copies, waits for them, and re-layouts: 18.7 us -> none  [decode(): reshaped * block_scale[None, :, :, :, None]]
    concatenate x2 -> x0, local copies, waits for them, and re-layouts: 8.9 us -> none  [the longest x1 8.04 us: combine_second(): jnp.concatenate([direct[..., :points] + crossed[..., points:], direct[......]
    unnamed x11 -> x22, local copies, waits for them, and re-layouts: 1.76 us -> 8.32 us
  transfers between devices with their start and end apart: 3 -> 3, of which waited for: 3 -> 2; matrix products, arithmetic and copies ran while one was open for 9% -> 0% of each run, Pallas kernels for 0% -> 8%
where the time goes in v1:
time: 123 us
  blocking collectives  65.8 us (53%)
  Pallas kernels  31.9 us (26%)
  waiting for transfers between devices  10.2 us (8%)
  local copies, waits for them, and re-layouts  9.42 us (8%)
  starting transfers between devices  5.13 us (4%)
    all_to_all x1, blocking collectives, on_device(): lax.all_to_all(summed.reshape(64, 2 * 16, rows), FREQ + ('zh', 'x'), 0, 0...  29.7 us
    all_to_all x1, blocking collectives, on_device(): own = lax.all_to_all(shares, ROWS, 0, 0, tiled=True).reshape(16 * rows, 128)  26.7 us
    all_to_all x1, blocking collectives, on_device(): returned = lax.all_to_all(spectra, FREQ, 0, 0, tiled=True)  9.4 us
    unnamed x22, local copies, waits for them, and re-layouts  8.32 us
    pallas_call x2, Pallas kernels, first_product(): pl.pallas_call(first_kernel, grid_spec=pltpu.PrefetchScalarGridSpec(num_s...  7.64 us
    all_to_all x1, waiting for transfers between devices, on_device(): samples = lax.all_to_all(focused, FREQ, 0, 0, tiled=True)  6.82 us
    pallas_call x1, Pallas kernels, second_product(): pl.pallas_call(second_kernel, grid_spec=pltpu.PrefetchScalarGridSpec(num_...  6.63 us
    pallas_call x1, Pallas kernels, final(): pl.pallas_call(final_kernel, grid=(8,), in_specs=[whole(a) for a in args]...  6.06 us
  transfers between devices with their start and end apart: 3, of which 2 were waited for; matrix products, arithmetic and copies ran while one was open for 0% of the time, Pallas kernels for 8%

profile of v1, /device:TPU:0, one launch (start us, length us, event | category | flops | bytes accessed | tf_op | source)
XLA Modules:
  0.0 123.0 jit_solution(6216901978495660859)
XLA Ops:
  0.0 0.0 copy-start.8
  0.0 1.1 broadcast_in_dim.14
  1.1 26.7 %all_to_all.20 = bf16[16,288,128]{2,1,0:T(8,128)(2,1)S(1)} all-to-all(bf16[16,288,128]{2,1,0:T(8,128)(2,1)S(1)} %bitcast.10), channel_id=1, replica_groups=mesh['y'=4,'zl'=2,'zh'=2,'x'=4,'c'=2] {'zh','x','c'}, dimensions={0} | all-to-all | bytes 2359296 | tf_op jit(solution)/shard_map/all_to_all | solution.py:295
  27.8 0.1 collective-permute-start
  27.9 0.0 copy-done.8
  27.9 0.2 copy.11.scale_ref
  28.1 0.0 copy-start.2
  28.1 4.0 %copy-done.2 = bf16[2,2,288,4608]{3,2,1,0:T(8,128)(2,1)S(1)} copy-done((bf16[2,2,288,4608]{3,2,1,0:T(8,128)(2,1)S(1)}, bf16[2,2,288,4608]{3,2,1,0:T(8,128)(2,1)}, u32[]{:S(2)}) %copy-start.2) | copy-done | bytes 10616856
  32.1 5.8 %decode.1.dec_ref = bf16[2,2,288,4608]{3,2,1,0:T(8,128)(2,1)S(1)} custom-call(bf16[2,2,288,4608]{3,2,1,0:T(8,128)(2,1)S(1)} %copy-done.2, f32[2,288,36]{2,1,0:T(8,128)S(1)} %copy.11.scale_ref), custom_call_target="tpu_custom_call" | custom-call | flops 5308416 | bytes 21233664 | tf_op jit(solution)/shard_map/decode/pallas_call | solution.py:71
  37.9 0.0 copy-start
  37.9 4.1 %first_product.2.rest_0_ = bf16[8,2,16,288]{3,2,1,0:T(8,128)(2,1)} custom-call(s32[1]{0:T(128)} %bitcast.pick_ref.core_ref, bf16[2,2,288,4608]{3,2,1,0:T(8,128)(2,1)S(1)} %decode.1.dec_ref, bf16[4608,128]{1,0:T(8,128)(2,1)S(1)} %bitcast.8), custom_call_target="tpu_custom_call" | custom-call | flops 679477248 | bytes 5308416 | tf_op jit(solution)/shard_map/first_product/pallas_call | solution.py:120
  42.0 0.0 copy-start.9
  42.0 0.0 copy-start.3
  42.0 0.0 copy-start.4
  42.0 0.0 copy-start.7
  42.0 0.0 collective-permute-done.focus_ref
  42.1 0.0 copy-done
  42.1 0.0 copy-start.6
  42.1 3.5 %first_product.3 = bf16[8,2,16,288]{3,2,1,0:T(8,128)(2,1)} custom-call(s32[1]{0:T(128)S(6)} %sub.3.pick_ref, bf16[2,2,288,4608]{3,2,1,0:T(8,128)(2,1)S(1)} %decode.1.dec_ref, bf16[4608,128]{1,0:T(8,128)(2,1)S(1)} %collective-permute-done.focus_ref, bf16[8,2,16,288]{3,2,1,0:T(8,128)(2,1)} %first_product.2.rest_0_), custom_call_target="tpu_custom_call", output_to_operand_aliasing={{}: (3, {})} | custom-call | flops 679477248 | bytes 5308416 | tf_op jit(solution)/shard_map/first_product/pallas_call | solution.py:120
  45.6 4.9 %all-to-all-start.1 = ((bf16[8,2,16,288]{3,2,1,0:T(8,128)(2,1)}), bf16[8,2,16,288]{3,2,1,0:T(8,128)(2,1)S(1)}, u32[]{:S(2)}, u32[]{:S(2)}) async-start(bf16[8,2,16,288]{3,2,1,0:T(8,128)(2,1)} %first_product.3), calls=%async_computation.1 | async-start | bytes 393216 | tf_op jit(solution)/shard_map/all_to_all | solution.py:300
  50.5 0.0 copy-done.9
  50.5 0.1 copy.12.cut_ref
  50.6 6.8 %all-to-all-done.1.in_ref = bf16[8,2,16,288]{3,2,1,0:T(8,128)(2,1)S(1)} async-done(((bf16[8,2,16,288]{3,2,1,0:T(8,128)(2,1)}), bf16[8,2,16,288]{3,2,1,0:T(8,128)(2,1)S(1)}, u32[]{:S(2)}, u32[]{:S(2)}) %all-to-all-start.1) | async-done | bytes 147488 | tf_op jit(solution)/shard_map/all_to_all | solution.py:300
  57.5 0.0 copy-done.3
  57.5 0.0 copy-done.4
  57.5 0.0 copy-done.7
  57.5 0.0 copy-done.6
  57.5 5.8 %mute.1 = bf16[8,2,16,288]{3,2,1,0:T(8,128)(2,1)S(1)} custom-call(s32[1]{0:T(128)} %bitcast.1.group_ref, bf16[8,2,16,288]{3,2,1,0:T(8,128)(2,1)S(1)} %all-to-all-done.1.in_ref, s32[288,64]{1,0:T(8,128)S(1)} %copy.12.cut_ref, bf16[256,512]{1,0:T(8,128)(2,1)S(1)} %copy-done.4, bf16[2,128,1024]{2,1,0:T(8,128)(2,1)S(1)} %copy-done.3, ...), custom_call_target="tpu_custom_call" | custom-call | flops 1207959552 | bytes 4194304 | tf_op jit(solution)/shard_map/mute/pallas_call | solution.py:181
  63.3 9.4 %all_to_all.21.ret_ref = bf16[8,2,16,288]{3,2,1,0:T(8,128)(2,1)S(1)} all-to-all(bf16[8,2,16,288]{3,2,1,0:T(8,128)(2,1)S(1)} %mute.1), channel_id=1, replica_groups=mesh['y'=4,'zl'=2,'zh'=2,'x'=4,'c'=2] {'y','zl'}, dimensions={0} | all-to-all | bytes 294912 | tf_op jit(solution)/shard_map/all_to_all | solution.py:302
  72.7 0.0 copy-start.1
  72.7 4.0 %copy-done.1 = bf16[2,2,288,4608]{3,2,1,0:T(8,128)(2,1)S(1)} copy-done((bf16[2,2,288,4608]{3,2,1,0:T(8,128)(2,1)S(1)}, bf16[2,2,288,4608]{3,2,1,0:T(8,128)(2,1)}, u32[]{:S(2)}) %copy-start.1) | copy-done | bytes 10616856
  76.7 6.6 %second_product.1 = (bf16[8,8,2,16,288]{4,3,2,1,0:T(8,128)(2,1)S(1)}, bf16[8,8,2,16,288]{4,3,2,1,0:T(8,128)(2,1)S(1)}) custom-call(s32[1]{0:T(128)} %bitcast.pick_ref.core_ref, bf16[8,2,16,288]{3,2,1,0:T(8,128)(2,1)S(1)} %all_to_all.21.ret_ref, bf16[2,2,288,4608]{3,2,1,0:T(8,128)(2,1)S(1)} %copy-done.1), custom_call_target="tpu_custom_call" | custom-call | flops 1358954496 | bytes 13271040 | tf_op jit(solution)/shard_map/second_product/pallas_call | solution.py:228
  83.3 0.1 collective-permute-start.1
  83.4 3.4 %collective-permute-done.1 = bf16[8,8,2,16,288]{4,3,2,1,0:T(8,128)(2,1)S(1)} collective-permute-done((bf16[8,8,2,16,288]{4,3,2,1,0:T(8,128)(2,1)S(1)}, bf16[8,8,2,16,288]{4,3,2,1,0:T(8,128)(2,1)S(1)}, u32[]{:S(2)}, u32[]{:S(2)}) %collective-permute-start.1) | collective-permute-done | bytes 1179680 | tf_op jit(solution)/shard_map/ppermute | solution.py:304
  86.8 0.4 add_convert_fusion
  87.2 0.0 copy-start.5
  87.3 29.7 %all_to_all.22 = bf16[64,32,288]{2,1,0:T(8,128)(2,1)S(1)} all-to-all(bf16[64,32,288]{2,1,0:T(8,128)(2,1)S(1)} %bitcast.9), channel_id=1, replica_groups=mesh['y'=4,'zl'=2,'zh'=2,'x'=4,'c'=2] {'y','zl','zh','x'}, dimensions={0} | all-to-all | bytes 2359296 | tf_op jit(solution)/shard_map/all_to_all | solution.py:306
  116.9 0.0 copy-done.5
  117.0 6.1 %final.1 = f32[8,288,1024]{2,1,0:T(8,128)} custom-call(bf16[8,8,32,288]{3,2,1,0:T(8,128)(2,1)S(1)} %bitcast.6, s32[8,288]{1,0:T(8,128)S(1)} %copy-done.5, bf16[256,512]{1,0:T(8,128)(2,1)S(1)} %copy-done.4, bf16[2,128,1024]{2,1,0:T(8,128)(2,1)S(1)} %copy-done.3), custom_call_target="tpu_custom_call" | custom-call | flops 603979776 | bytes 12582912 | tf_op jit(solution)/shard_map/final/pallas_call | solution.py:273
Async XLA Ops:
  0.0 27.9 %copy-start.8 = (f32[2,288,36]{1,0,2:T(2,128)S(1)}, f32[2,288,36]{1,0,2:T(2,128)}, u32[]{:S(2)}) copy-start(f32[2,288,36]{1,0,2:T(2,128)} %param.10) | copy-start | bytes 248836
  27.8 14.2 %collective-permute-start = (bf16[4608,128]{1,0:T(8,128)(2,1)S(1)}, bf16[4608,128]{1,0:T(8,128)(2,1)S(1)}, u32[]{:S(2)}, u32[]{:S(2)}) collective-permute-start(bf16[4608,128]{1,0:T(8,128)(2,1)S(1)} %bitcast.7), channel_id=1, source_target_pairs={{0,1},{1,0},{2,3},{3,2},{4,5},{5,4},{6,7},{7,6},{8,9},{9,8},{10,11... | collective-permute-start | bytes 3538952 | tf_op jit(solution)/shard_map/ppermute | solution.py:297
  28.1 4.0 %copy-start.2 = (bf16[2,2,288,4608]{3,2,1,0:T(8,128)(2,1)S(1)}, bf16[2,2,288,4608]{3,2,1,0:T(8,128)(2,1)}, u32[]{:S(2)}) copy-start(bf16[2,2,288,4608]{3,2,1,0:T(8,128)(2,1)} %refl_ref.1) | copy-start | bytes 31850500
  37.9 4.2 %copy-start = (bf16[2,2,288,4608]{3,2,1,0:T(8,128)(2,1)}, bf16[2,2,288,4608]{3,2,1,0:T(8,128)(2,1)S(1)}, u32[]{:S(2)}) copy-start(bf16[2,2,288,4608]{3,2,1,0:T(8,128)(2,1)S(1)} %decode.1.dec_ref) | copy-start | bytes 31850500
  42.0 8.5 %copy-start.9 = (s32[288,64]{0,1:T(8,128)S(1)}, s32[288,64]{0,1:T(8,128)}, u32[]{:S(2)}) copy-start(s32[288,64]{0,1:T(8,128)} %param.12) | copy-start | bytes 221188
  42.0 15.4 %copy-start.3 = (bf16[2,128,1024]{2,1,0:T(8,128)(2,1)S(1)}, bf16[2,128,1024]{2,1,0:T(8,128)(2,1)}, u32[]{:S(2)}) copy-start(bf16[2,128,1024]{2,1,0:T(8,128)(2,1)} %constant.26.clone.inv_ref) | copy-start | bytes 1572868
  42.0 15.4 %copy-start.4 = (bf16[256,512]{1,0:T(8,128)(2,1)S(1)}, bf16[256,512]{1,0:T(8,128)(2,1)}, u32[]{:S(2)}) copy-start(bf16[256,512]{1,0:T(8,128)(2,1)} %constant.27.clone.spread_ref) | copy-start | bytes 786436
  42.0 15.4 %copy-start.7 = (bf16[1024,128]{1,0:T(8,128)(2,1)S(1)}, bf16[1024,128]{1,0:T(8,128)(2,1)}, u32[]{:S(2)}) copy-start(bf16[1024,128]{1,0:T(8,128)(2,1)} %constant.28.clone.fwd_ref) | copy-start | bytes 786436
  42.1 15.4 %copy-start.6 = (bf16[8,128,256]{2,1,0:T(8,128)(2,1)S(1)}, bf16[8,128,256]{2,1,0:T(8,128)(2,1)}, u32[]{:S(2)}) copy-start(bf16[8,128,256]{2,1,0:T(8,128)(2,1)} %constant.29.clone.back_ref) | copy-start | bytes 1572868
  45.6 11.9 %all-to-all-start.1 = ((bf16[8,2,16,288]{3,2,1,0:T(8,128)(2,1)}), bf16[8,2,16,288]{3,2,1,0:T(8,128)(2,1)S(1)}, u32[]{:S(2)}, u32[]{:S(2)}) async-start(bf16[8,2,16,288]{3,2,1,0:T(8,128)(2,1)} %first_product.3), calls=%async_computation.1 | async-start | bytes 393216 | tf_op jit(solution)/shard_map/all_to_all | solution.py:300
  72.7 4.0 %copy-start.1 = (bf16[2,2,288,4608]{3,2,1,0:T(8,128)(2,1)S(1)}, bf16[2,2,288,4608]{3,2,1,0:T(8,128)(2,1)}, u32[]{:S(2)}) copy-start(bf16[2,2,288,4608]{3,2,1,0:T(8,128)(2,1)} %copy-done) | copy-start | bytes 31850500
  83.3 3.5 %collective-permute-start.1 = (bf16[8,8,2,16,288]{4,3,2,1,0:T(8,128)(2,1)S(1)}, bf16[8,8,2,16,288]{4,3,2,1,0:T(8,128)(2,1)S(1)}, u32[]{:S(2)}, u32[]{:S(2)}) collective-permute-start(bf16[8,8,2,16,288]{4,3,2,1,0:T(8,128)(2,1)S(1)} %get-tuple-element.8), channel_id=1, source_target_pairs={{0,1},{1,0},{2,3},{3,2},{4,5},{5,4},{6,7},{7,6},{8,9},{9,8},{10,11... | collective-permute-start | bytes 3538952 | tf_op jit(solution)/shard_map/ppermute | solution.py:304
  87.2 29.7 %copy-start.5 = (s32[8,288]{1,0:T(8,128)S(1)}, s32[8,288]{1,0:T(8,128)}, u32[]{:S(2)}) copy-start(s32[8,288]{1,0:T(8,128)} %cut_ref.2) | copy-start | bytes 27652

commit v2 on v1

v2 whole, which is shorter than its diff:
```python
import functools
import math

import jax
import jax.numpy as jnp
import numpy as np
from jax import lax
from jax.experimental import pallas as pl
from jax.experimental.pallas import tpu as pltpu
from jax.sharding import Mesh
from jax.sharding import PartitionSpec as P

NT = 1024
LOWBIN = 24
FREQ = ("y", "zl")
ROWS = ("zh", "x", "c")
SWAP = ((0, 1), (1, 0))
BF = jnp.bfloat16
F32 = jnp.float32
MB = 1 << 20
VL1 = 20 * MB
VL2 = 26 * MB
KSTEP = 1152
AHEAD = 8


def tables(freq_total):
    phases = (
        (LOWBIN + np.arange(freq_total))[:, None] * np.arange(NT)[None, :] % NT
    ) * (2.0 * math.pi / NT)
    inward = 1.0 / math.sqrt(2.0 * freq_total)
    outward = 2.0 / (NT * inward)
    rows = np.stack([np.cos(phases), -np.sin(phases)], 1).reshape(2 * freq_total, NT)
    return rows * inward, rows * outward


def split(table):
    upper = table.astype(BF)
    lower = (table - upper.astype(np.float64)).astype(BF)
    return upper, lower


def constants(freq_total, group):
    inverse, forward = tables(freq_total)
    rows = 2 * freq_total
    upper, lower = split(inverse)
    pair = np.concatenate([upper, lower], 0)
    zero = np.zeros_like(pair)
    inv = np.stack([np.concatenate([pair, zero], 0), np.concatenate([zero, pair], 0)])
    spread = np.zeros((rows * group, 2 * rows * group), BF)
    for q in range(rows):
        for p in range(group):
            for h in range(2):
                spread[q * group + p, p * 2 * rows + h * rows + q] = 1
    fwd = np.zeros((NT, 128), BF)
    fwd[:, :rows] = forward.T.astype(BF)
    back = np.zeros((group, 128, rows * group), BF)
    for q in range(rows):
        for p in range(group):
            back[p, q, q * group + p] = 1
    mixed = spread.reshape(group, 2, 2, group, -1).transpose(1, 2, 0, 3, 4).reshape(spread.shape)
    return inv, spread, fwd, back, mixed


def decode_kernel(refl_ref, scale_ref, out_ref):
    blocks = scale_ref.shape[-1]
    for b in range(blocks):
        scale = scale_ref[0, :, b : b + 1]
        for k in range(2):
            part = refl_ref[k, 0, :, b * 128 : (b + 1) * 128].astype(F32)
            out_ref[k, 0, :, b * 128 : (b + 1) * 128] = (part * scale).astype(BF)


def decode(refl, scale):
    _, freqs, rows, cols = refl.shape
    step = 48
    return pl.pallas_call(
        decode_kernel,
        grid=(freqs, rows // step),
        in_specs=[
            pl.BlockSpec((2, 1, step, cols), lambda f, s: (0, f, s, 0)),
            pl.BlockSpec((1, step, scale.shape[-1]), lambda f, s: (f, s, 0)),
        ],
        out_specs=pl.BlockSpec((2, 1, step, cols), lambda f, s: (0, f, s, 0)),
        out_shape=jax.ShapeDtypeStruct(refl.shape, BF),
        compiler_params=pltpu.CompilerParams(vmem_limit_bytes=52 * MB),
        cost_estimate=pl.CostEstimate(
            flops=refl.size, bytes_accessed=4 * refl.size, transcendentals=0
        ),
        name="decode",
    )(refl, scale)


def turn(sums, rows):
    direct = sums[:rows]
    crossed = pltpu.roll(sums[rows:], 64, 1)
    lane = lax.broadcasted_iota(jnp.int32, direct.shape, 1)
    both = direct + jnp.where(lane < 64, -crossed, crossed)
    turned = both.T.reshape(2, 8, 8, rows)
    return jnp.concatenate([turned[0], turned[1]], 1).astype(BF)


def first_own_kernel(core_ref, group_ref, dec_ref, focus_ref, out_ref, own_ref, other_ref, acc_ref, sem):
    f = core_ref[0]
    _, rows, cols = own_ref.shape
    spans = [slice(k * KSTEP, (k + 1) * KSTEP) for k in range(cols // KSTEP)]
    copies = []
    for ref, which in ((own_ref, f), (other_ref, 1 - f)):
        for here in spans:
            copies.append(
                pltpu.make_async_copy(
                    dec_ref.at[:, which, :, here], ref.at[:, :, here], sem.at[len(copies)]
                )
            )
    for copy in copies[:AHEAD]:
        copy.start()
    for k, here in enumerate(spans):
        copies[k].wait()
        if k + AHEAD < len(copies):
            copies[k + AHEAD].start()
        part = jnp.dot(
            own_ref[:, :, here].reshape(2 * rows, KSTEP),
            focus_ref[here],
            preferred_element_type=F32,
        )
        if k == 0:
            acc_ref[...] = part
        else:
            acc_ref[...] += part
    for copy in copies[len(spans) + AHEAD :]:
        copy.start()
    out_ref[:, f] = turn(acc_ref[...], rows)
    for copy in copies[len(spans) :]:
        copy.wait()


def first_other_kernel(core_ref, dec_ref, focus_ref, half_ref, out_ref, acc_ref):
    f = 1 - core_ref[0]
    _, rows, cols = dec_ref.shape
    for k in range(cols // KSTEP):
        here = slice(k * KSTEP, (k + 1) * KSTEP)
        part = jnp.dot(
            dec_ref[:, :, here].reshape(2 * rows, KSTEP),
            focus_ref[here],
            preferred_element_type=F32,
        )
        if k == 0:
            acc_ref[...] = part
        else:
            acc_ref[...] += part
    out_ref[:, f] = turn(acc_ref[...], rows)
    out_ref[:, 1 - f] = half_ref[:, 1 - f]


VMEM = pl.BlockSpec(memory_space=pltpu.VMEM)
SMEM = pl.BlockSpec(memory_space=pltpu.SMEM)


def first_own(core, group, decoded, focus):
    _, freqs, rows, cols = decoded.shape
    held = jax.ShapeDtypeStruct((2, rows, cols), BF)
    return pl.pallas_call(
        first_own_kernel,
        in_specs=[SMEM, SMEM, pl.BlockSpec(memory_space=pltpu.HBM), VMEM],
        out_specs=[VMEM] * 3,
        scratch_shapes=[
            pltpu.VMEM((2 * rows, 128), F32),
            pltpu.SemaphoreType.DMA((2 * cols // KSTEP,)),
        ],
        out_shape=[jax.ShapeDtypeStruct((8, freqs, 16, rows), BF), held, held],
        compiler_params=pltpu.CompilerParams(vmem_limit_bytes=VL1),
        cost_estimate=pl.CostEstimate(
            flops=4 * rows * cols * 128, bytes_accessed=8 * rows * cols, transcendentals=0
        ),
        name="first_own",
    )(core, group, decoded, focus)


def first_other(core, held, focus, half):
    _, rows, cols = held.shape
    return pl.pallas_call(
        first_other_kernel,
        in_specs=[SMEM, VMEM, VMEM, VMEM],
        out_specs=VMEM,
        scratch_shapes=[pltpu.VMEM((2 * rows, 128), F32)],
        out_shape=jax.ShapeDtypeStruct(half.shape, BF),
        compiler_params=pltpu.CompilerParams(vmem_limit_bytes=VL1),
        cost_estimate=pl.CostEstimate(
            flops=4 * rows * cols * 128, bytes_accessed=4 * rows * cols, transcendentals=0
        ),
        name="first_other",
    )(core, held, focus, half)


def mute_kernel(group_ref, in_ref, cut_ref, spread_ref, inv_ref, fwd_ref, back_ref, out_ref, wide_ref):
    rows = in_ref.shape[-1]
    turned = in_ref[...].reshape(256, rows).astype(F32).T.astype(BF)
    wide = jnp.dot(turned, spread_ref[...], preferred_element_type=F32)
    for q in range(4):
        wide_ref[q] = wide[:, q * 128 : (q + 1) * 128].astype(BF)
    own = pl.ds(pl.multiple_of(group_ref[0] * 8, 8), 8)
    edge = cut_ref[own].astype(F32).T
    total = None
    for p in range(8):
        traces = jnp.dot(wide_ref[p // 2], inv_ref[p % 2], preferred_element_type=F32)
        cut = edge[:, p : p + 1].astype(jnp.int32)
        time = lax.broadcasted_iota(jnp.int32, traces.shape, 1)
        kept = jnp.where(time < cut, traces, 0.0).astype(BF)
        ret = jnp.dot(kept, fwd_ref[...], preferred_element_type=F32).astype(BF)
        part = jnp.dot(ret, back_ref[p], preferred_element_type=F32)
        total = part if total is None else total + part
    out_ref[...] = total.T.reshape(8, 2, 16, rows).astype(BF)


def mute(group, samples, cut, spread, inv, fwd, back):
    rows = samples.shape[-1]
    return pl.pallas_call(
        mute_kernel,
        in_specs=[SMEM] + [VMEM] * 6,
        out_specs=VMEM,
        scratch_shapes=[pltpu.VMEM((4, rows, 128), BF)],
        out_shape=jax.ShapeDtypeStruct(samples.shape, BF),
        compiler_params=pltpu.CompilerParams(vmem_limit_bytes=24 * MB),
        cost_estimate=pl.CostEstimate(
            flops=8 * rows * NT * 512, bytes_accessed=4 * MB, transcendentals=0
        ),
        name="mute",
    )(group, samples, cut, spread, inv, fwd, back)


def second_kernel(base, core_ref, ret_ref, own_ref, other_ref, keep_ref, send_ref, lhs_ref):
    rows = own_ref.shape[1]
    even = core_ref[0] == 0

    @pl.when(pl.program_id(0) == 0)
    def _():
        for f in range(2):
            direct = ret_ref[:, f].astype(F32)
            crossed = jnp.concatenate([direct[:, 8:], -direct[:, :8]], 1)
            lhs_ref[f] = jnp.concatenate(
                [direct.reshape(128, rows), crossed.reshape(128, rows)], 1
            ).astype(BF)

    parts = []
    step = 4 * rows
    here = pl.ds(pl.multiple_of((base + pl.program_id(0)) * step, 128), step)
    for k, ref in enumerate((own_ref, other_ref)):
        f = core_ref[0] if k == 0 else 1 - core_ref[0]
        parts.append(
            jnp.dot(
                lhs_ref[f],
                ref[:, :, here].reshape(2 * rows, step),
                preferred_element_type=F32,
            ).reshape(8, 2, 8, step)
        )
    parts = [
        jnp.where(even, parts[f], parts[1 - f])[:, k] for f in range(2) for k in range(2)
    ]
    lane = lax.broadcasted_iota(jnp.int32, (8, 8, 128), 2)
    low, first = lane < 64, (lane // 32) % 2 == 0
    pieces = []
    for v in range(4 * rows // 128):
        a, b, c, d = (x[:, :, v * 128 : (v + 1) * 128] for x in parts)
        a, c = jnp.where(low, a, pltpu.roll(c, 64, 2)), jnp.where(low, pltpu.roll(a, 64, 2), c)
        b, d = jnp.where(low, b, pltpu.roll(d, 64, 2)), jnp.where(low, pltpu.roll(b, 64, 2), d)
        a, b = jnp.where(first, a, pltpu.roll(b, 32, 2)), jnp.where(first, pltpu.roll(a, 96, 2), b)
        c, d = jnp.where(first, c, pltpu.roll(d, 32, 2)), jnp.where(first, pltpu.roll(c, 96, 2), d)
        pieces += [a, b, c, d]
    per = rows // 32
    for j in range(2):
        left = jnp.concatenate(pieces[2 * j * per : (2 * j + 1) * per], 1)
        right = jnp.concatenate(pieces[(2 * j + 1) * per : (2 * j + 2) * per], 1)
        keep_ref[:, j] = jnp.where(even, left, right).astype(BF)
        send_ref[:, j] = jnp.where(even, right, left).astype(BF)


def second_product(core, returned, own, other, part):
    freqs = 2
    _, rows, cols = own.shape
    step = 4 * rows
    packed = rows // 32 * 8
    shape = jax.ShapeDtypeStruct((8, 4, packed, 128), BF)
    spec = pl.BlockSpec((8, 2, packed, 128), lambda k, core: (0, k, 0, 0))
    return pl.pallas_call(
        functools.partial(second_kernel, 2 * part),
        grid_spec=pltpu.PrefetchScalarGridSpec(
            num_scalar_prefetch=1,
            grid=(cols // step // 2,),
            in_specs=[
                pl.BlockSpec((8, freqs, 16, rows), lambda k, core: (0, 0, 0, 0)),
                pl.BlockSpec(memory_space=pltpu.VMEM),
                pl.BlockSpec(memory_space=pltpu.VMEM),
            ],
            out_specs=[spec, spec],
            scratch_shapes=[pltpu.VMEM((2, 128, 2 * rows), BF)],
        ),
        out_shape=[shape, shape],
        compiler_params=pltpu.CompilerParams(vmem_limit_bytes=VL2),
        cost_estimate=pl.CostEstimate(
            flops=4 * rows * cols * 128, bytes_accessed=5 * rows * cols, transcendentals=0
        ),
        name="second_product",
    )(core, returned, own, other)


def merge_kernel(a_ref, b_ref, c_ref, d_ref, out_ref):
    for g in range(8):
        out_ref[g, :4] = (a_ref[g].astype(F32) + b_ref[g].astype(F32)).astype(BF)
        out_ref[g, 4:] = (c_ref[g].astype(F32) + d_ref[g].astype(F32)).astype(BF)


def merge(*parts):
    return pl.pallas_call(
        merge_kernel,
        in_specs=[VMEM] * 4,
        out_specs=VMEM,
        out_shape=jax.ShapeDtypeStruct((8, 8) + parts[0].shape[2:], BF),
        compiler_params=pltpu.CompilerParams(vmem_limit_bytes=8 * MB),
        name="merge",
    )(*parts)


def final_kernel(in_ref, cut_ref, spread_ref, inv_ref, out_ref, wide_ref, slab_ref, sem):
    per = in_ref.shape[2] // 8
    total = in_ref[:, 0].astype(F32)
    for j in range(1, 8):
        total += in_ref[:, j].astype(F32)
    slabs = []
    for k in range(per):
        turned = total[:, k * 8 : (k + 1) * 8].reshape(64, 128).T
        slabs.append(jnp.concatenate([turned[t * 32 : (t + 1) * 32] for t in range(4)], 1))
    turned = jnp.concatenate(slabs, 0).astype(BF)
    wide = jnp.dot(turned, spread_ref[...], preferred_element_type=F32)
    for q in range(4):
        wide_ref[q] = wide[:, q * 128 : (q + 1) * 128].astype(BF)
    edge = cut_ref[...].astype(F32).T

    def out(p):
        return pltpu.make_async_copy(slab_ref.at[p], out_ref.at[p], sem.at[p])

    for p in range(8):
        traces = jnp.dot(wide_ref[p // 2], inv_ref[p % 2], preferred_element_type=F32)
        cut = edge[:, p : p + 1].astype(jnp.int32)
        time = lax.broadcasted_iota(jnp.int32, traces.shape, 1)
        slab_ref[p] = jnp.where(time < cut, traces, 0.0)
        out(p).start()
    for p in range(8):
        out(p).wait()


def final(partials, cut, spread, inv):
    rows = cut.shape[1]
    args = (partials, cut, spread, inv)
    return pl.pallas_call(
        final_kernel,
        in_specs=[VMEM] * 4,
        out_specs=pl.BlockSpec(memory_space=pltpu.HBM),
        scratch_shapes=[
            pltpu.VMEM((4, rows, 128), BF),
            pltpu.VMEM((8, rows, NT), F32),
            pltpu.SemaphoreType.DMA((8,)),
        ],
        out_shape=jax.ShapeDtypeStruct((8, rows, NT), F32),
        compiler_params=pltpu.CompilerParams(vmem_limit_bytes=24 * MB),
        cost_estimate=pl.CostEstimate(
            flops=8 * rows * NT * 256, bytes_accessed=12 * MB, transcendentals=0
        ),
        name="final",
    )(*args)


def on_device(refl, refl_scale, focus, first_mute, second_mute):
    _, freqs, rows, _ = refl.shape
    core = lax.axis_index("c").astype(jnp.int32)[None]
    group = lax.axis_index(FREQ).astype(jnp.int32)[None]
    inv, spread, fwd, back, mixed = (jnp.asarray(a) for a in constants(8 * freqs, 8))

    shares = jnp.broadcast_to(focus[None], (8, 2, rows, 128)).reshape(16, rows, 128)
    own = lax.all_to_all(shares, ROWS, 0, 0, tiled=True).reshape(16 * rows, 128)
    decoded = pltpu.with_memory_space_constraint(decode(refl, refl_scale), pltpu.HBM)
    other = lax.ppermute(own, "c", SWAP)
    half, dec_own, dec_other = first_own(core, group, decoded, own)
    focused = first_other(core, dec_other, other, half)
    samples = lax.all_to_all(focused, FREQ, 0, 0, tiled=True)
    spectra = mute(group, samples, first_mute.T, spread, inv, fwd, back)
    returned = lax.all_to_all(spectra, FREQ, 0, 0, tiled=True)
    keep_a, send_a = second_product(core, returned, dec_own, dec_other, 0)
    got_a = lax.ppermute(send_a, "c", SWAP)
    keep_b, send_b = second_product(core, returned, dec_own, dec_other, 1)
    got_b = lax.ppermute(send_b, "c", SWAP)
    summed = merge(keep_a, got_a, keep_b, got_b)
    partials = lax.all_to_all(
        summed.reshape(64, -1, 128), FREQ + ("zh", "x"), 0, 0, tiled=True
    )
    return final(partials.reshape(8, 8, -1, 128), second_mute, mixed, inv)


def solution(mesh):
    fine = Mesh(mesh.devices.reshape(4, 2, 2, 4, 2), ("y", "zl", "zh", "x", "c"))
    in_specs = (
        P(None, FREQ, ROWS, None),
        P(FREQ, ROWS, None),
        P(FREQ, ROWS, None),
        P(ROWS, None),
        P(FREQ, ROWS),
    )
    return jax.shard_map(
        on_device, mesh=fine, in_specs=in_specs, out_specs=P(FREQ, ROWS, None), check_vma=False
    )
```

time: 123 us -> 112 us (0.911)
  waiting for transfers between devices: 10.2 us -> 1.63 us
  blocking collectives: 65.8 us -> 73.5 us
  local copies, waits for them, and re-layouts: 9.42 us -> 2.15 us
  starting transfers between devices: 5.13 us -> 0.75 us
  Pallas kernels: 31.9 us -> 33.2 us
    pallas_call x1, Pallas kernels: 5.77 us -> 13.8 us  [decode(): pl.pallas_call(decode_kernel, grid=(freqs, rows // step), in_specs=[pl.Bl...]
    all_to_all x1 -> x2, blocking collectives: 29.7 us -> 37.3 us  [the longest x1 25.7 us: on_device(): lax.all_to_all(summed.reshape(64, -1, 128), FREQ + ('zh', 'x'), 0, 0, til...]
    unnamed x22 -> x15, local copies, waits for them, and re-layouts: 8.32 us -> 1.09 us
    all_to_all x1 -> x0, waiting for transfers between devices: 6.82 us -> none  [on_device(): samples = lax.all_to_all(focused, FREQ, 0, 0, tiled=True)]
    pallas_call x5 -> x7, Pallas kernels: 26.1 us -> 19.4 us  [the longest x1 4.62 us: first_own(): pl.pallas_call(first_own_kernel, in_specs=[SMEM, SMEM, pl.BlockSpec(memor...]
    all_to_all x1 -> x0, starting transfers between devices: 4.93 us -> none  [on_device(): samples = lax.all_to_all(focused, FREQ, 0, 0, tiled=True)]
    ppermute x1 -> x2, waiting for transfers between devices: 3.4 us -> 1.63 us  [the longest x1 1.63 us: on_device(): got_a = lax.ppermute(send_a, 'c', SWAP)]
  transfers between devices with their start and end apart: 3 -> 3, of which waited for: 2 -> 1; matrix products, arithmetic and copies ran while one was open for 0% -> 1% of each run, Pallas kernels for 8% -> 18%
where the time goes in v2:
time: 112 us; the launch traced here: 111 us
  blocking collectives  73.5 us (66%)
  Pallas kernels  33.2 us (30%)
  local copies, waits for them, and re-layouts  2.15 us (2%)
  waiting for transfers between devices  1.63 us (1%)
    all_to_all x1, blocking collectives, on_device(): own = lax.all_to_all(shares, ROWS, 0, 0, tiled=True).reshape(16 * rows, 128)  26.7 us
    all_to_all x1, blocking collectives, on_device(): lax.all_to_all(summed.reshape(64, -1, 128), FREQ + ('zh', 'x'), 0, 0, til...  25.7 us
    pallas_call x1, Pallas kernels, decode(): pl.pallas_call(decode_kernel, grid=(freqs, rows // step), in_specs=[pl.Bl...  13.8 us
    all_to_all x1, blocking collectives, on_device(): samples = lax.all_to_all(focused, FREQ, 0, 0, tiled=True)  11.7 us
    all_to_all x1, blocking collectives, on_device(): returned = lax.all_to_all(spectra, FREQ, 0, 0, tiled=True)  9.41 us
    pallas_call x1, Pallas kernels, first_own(): pl.pallas_call(first_own_kernel, in_specs=[SMEM, SMEM, pl.BlockSpec(memor...  4.62 us
    pallas_call x1, Pallas kernels, final(): pl.pallas_call(final_kernel, in_specs=[VMEM] * 4, out_specs=pl.BlockSpec(...  4.53 us
    pallas_call x1, Pallas kernels, mute(): pl.pallas_call(mute_kernel, in_specs=[SMEM] + [VMEM] * 6, out_specs=VMEM,...  4.15 us
  transfers between devices with their start and end apart: 3, of which 1 were waited for; matrix products, arithmetic and copies ran while one was open for 1% of the time, Pallas kernels for 18%

profile of v2, /device:TPU:0, one launch (start us, length us, event | category | flops | bytes accessed | tf_op | source)
XLA Modules:
  0.0 111.4 jit_solution(10434708604777413626)
XLA Ops:
  0.0 1.1 broadcast_in_dim.14
  1.1 26.7 %all_to_all.20 = bf16[16,288,128]{2,1,0:T(8,128)(2,1)S(1)} all-to-all(bf16[16,288,128]{2,1,0:T(8,128)(2,1)S(1)} %bitcast.12), channel_id=1, replica_groups=mesh['y'=4,'zl'=2,'zh'=2,'x'=4,'c'=2] {'zh','x','c'}, dimensions={0} | all-to-all | bytes 2359296 | tf_op jit(solution)/shard_map/all_to_all | solution.py:379
  27.8 0.1 collective-permute-start
  27.9 1.0 copy.11.scale_ref
  29.0 13.8 %decode.1.dec_ref = bf16[2,2,288,4608]{3,2,1,0:T(8,128)(2,1)} custom-call(bf16[2,2,288,4608]{3,2,1,0:T(8,128)(2,1)} %refl_ref.1, f32[2,288,36]{2,1,0:T(8,128)S(1)} %copy.11.scale_ref), custom_call_target="tpu_custom_call" | custom-call | flops 5308416 | bytes 21233664 | tf_op jit(solution)/shard_map/decode/pallas_call | solution.py:77
  42.7 4.6 %first_own.1 = (bf16[8,2,16,288]{3,2,1,0:T(8,128)(2,1)S(1)}, bf16[2,288,4608]{2,1,0:T(8,128)(2,1)S(1)}, bf16[2,288,4608]{2,1,0:T(8,128)(2,1)S(1)}) custom-call(s32[1]{0:T(128)} %bitcast.core_ref, s32[1]{0:T(128)} %bitcast.1.group_ref, bf16[2,2,288,4608]{3,2,1,0:T(8,128)(2,1)} %decode.1.dec_ref, bf16[4608,128]{1,0:T(8,128)(2,1)S(1)} %bitcast.8), custom_call_target="tpu_custom_call" | custom-call | flops 679477248 | bytes 10616832 | tf_op jit(solution)/shard_map/first_own/pallas_call | solution.py:162
  47.4 0.0 copy-start
  47.4 0.0 copy-start.3
  47.4 0.0 copy-start.4
  47.4 0.0 copy-start.5
  47.4 0.0 copy-start.6
  47.4 0.0 collective-permute-done.focus_ref
  47.4 1.7 %first_other.1 = bf16[8,2,16,288]{3,2,1,0:T(8,128)(2,1)S(1)} custom-call(s32[1]{0:T(128)} %bitcast.core_ref, bf16[2,288,4608]{2,1,0:T(8,128)(2,1)S(1)} %get-tuple-element.12.dec_ref.other_ref, bf16[4608,128]{1,0:T(8,128)(2,1)S(1)} %collective-permute-done.focus_ref, bf16[8,2,16,288]{3,2,1,0:T(8,128)(2,1)S(1)} %get-tuple-element.13.half_ref), custom_call_target="tpu_custom_call" | custom-call | flops 679477248 | bytes 5308416 | tf_op jit(solution)/shard_map/first_other/pallas_call | solution.py:181
  49.2 11.7 %all_to_all.21.in_ref = bf16[8,2,16,288]{3,2,1,0:T(8,128)(2,1)S(1)} all-to-all(bf16[8,2,16,288]{3,2,1,0:T(8,128)(2,1)S(1)} %first_other.1), channel_id=1, replica_groups=mesh['y'=4,'zl'=2,'zh'=2,'x'=4,'c'=2] {'y','zl'}, dimensions={0} | all-to-all | bytes 294912 | tf_op jit(solution)/shard_map/all_to_all | solution.py:384
  60.8 0.0 copy-done
  60.8 0.0 copy-done.3
  60.8 0.0 copy-done.4
  60.8 0.0 copy-done.5
  60.8 0.0 copy-done.6
  60.8 4.2 %mute.1 = bf16[8,2,16,288]{3,2,1,0:T(8,128)(2,1)S(1)} custom-call(s32[1]{0:T(128)} %bitcast.1.group_ref, bf16[8,2,16,288]{3,2,1,0:T(8,128)(2,1)S(1)} %all_to_all.21.in_ref, s32[64,288]{1,0:T(8,128)S(1)} %bitcast.11, bf16[256,512]{1,0:T(8,128)(2,1)S(1)} %copy-done.5, bf16[2,128,1024]{2,1,0:T(8,128)(2,1)S(1)} %copy-done, bf16[1024,128]{1,0:T(8,128)(2,1)S(1)} %copy-done.6, ...), custom_call_target="tpu_custom_call" | custom-call | flops 1207959552 | bytes 4194304 | tf_op jit(solution)/shard_map/mute/pallas_call | solution.py:217
  65.0 9.4 %all_to_all.22.ret_ref = bf16[8,2,16,288]{3,2,1,0:T(8,128)(2,1)S(1)} all-to-all(bf16[8,2,16,288]{3,2,1,0:T(8,128)(2,1)S(1)} %mute.1), channel_id=1, replica_groups=mesh['y'=4,'zl'=2,'zh'=2,'x'=4,'c'=2] {'y','zl'}, dimensions={0} | all-to-all | bytes 294912 | tf_op jit(solution)/shard_map/all_to_all | solution.py:386
  74.4 2.0 %second_product.3 = (bf16[8,4,72,128]{3,2,1,0:T(8,128)(2,1)S(1)}, bf16[8,4,72,128]{3,2,1,0:T(8,128)(2,1)S(1)}) custom-call(s32[1]{0:T(128)} %bitcast.core_ref, bf16[8,2,16,288]{3,2,1,0:T(8,128)(2,1)S(1)} %all_to_all.22.ret_ref, bf16[2,288,4608]{2,1,0:T(8,128)(2,1)S(1)} %get-tuple-element.14.own_ref, bf16[2,288,4608]{2,1,0:T(8,128)(2,1)S(1)} %get-tuple-element.12.dec_ref.other_ref), custom_call_target="tpu_custom_call" | custom-call | flops 679477248 | bytes 6635520 | tf_op jit(solution)/shard_map/second_product/pallas_call | solution.py:284
  76.5 0.1 collective-permute-start.2
  76.5 2.1 %second_product.2 = (bf16[8,4,72,128]{3,2,1,0:T(8,128)(2,1)S(1)}, bf16[8,4,72,128]{3,2,1,0:T(8,128)(2,1)S(1)}) custom-call(s32[1]{0:T(128)} %bitcast.core_ref, bf16[8,2,16,288]{3,2,1,0:T(8,128)(2,1)S(1)} %all_to_all.22.ret_ref, bf16[2,288,4608]{2,1,0:T(8,128)(2,1)S(1)} %get-tuple-element.14.own_ref, bf16[2,288,4608]{2,1,0:T(8,128)(2,1)S(1)} %get-tuple-element.12.dec_ref.other_ref), custom_call_target="tpu_custom_call" | custom-call | flops 679477248 | bytes 6635520 | tf_op jit(solution)/shard_map/second_product/pallas_call | solution.py:284
  78.7 0.0 copy-start.1
  78.7 0.0 copy-start.2
  78.7 0.6 collective-permute-start.1
  79.2 0.0 collective-permute-done.2.d_ref
  79.2 1.6 %collective-permute-done.1.b_ref = bf16[8,4,72,128]{3,2,1,0:T(8,128)(2,1)S(1)} collective-permute-done((bf16[8,4,72,128]{3,2,1,0:T(8,128)(2,1)S(1)}, bf16[8,4,72,128]{3,2,1,0:T(8,128)(2,1)S(1)}, u32[]{:S(2)}, u32[]{:S(2)}) %collective-permute-start.1) | collective-permute-done | bytes 589856 | tf_op jit(solution)/shard_map/ppermute | solution.py:388
  80.9 0.3 merge.1
  81.1 25.7 %all_to_all.23 = bf16[64,72,128]{2,1,0:T(8,128)(2,1)S(1)} all-to-all(bf16[64,72,128]{2,1,0:T(8,128)(2,1)S(1)} %bitcast.10), channel_id=1, replica_groups=mesh['y'=4,'zl'=2,'zh'=2,'x'=4,'c'=2] {'y','zl','zh','x'}, dimensions={0} | all-to-all | bytes 2359296 | tf_op jit(solution)/shard_map/all_to_all | solution.py:392
  106.8 0.0 copy-done.1
  106.8 0.0 copy-done.2
  106.8 4.5 %final.1 = f32[8,288,1024]{2,1,0:T(8,128)} custom-call(bf16[8,8,72,128]{3,2,1,0:T(8,128)(2,1)S(1)} %bitcast.9, s32[8,288]{1,0:T(8,128)S(1)} %copy-done.2, bf16[256,512]{1,0:T(8,128)(2,1)S(1)} %copy-done.1, bf16[2,128,1024]{2,1,0:T(8,128)(2,1)S(1)} %copy-done), custom_call_target="tpu_custom_call" | custom-call | flops 603979776 | bytes 12582912 | tf_op jit(solution)/shard_map/final/pallas_call | solution.py:354
Async XLA Ops:
  27.8 19.6 %collective-permute-start = (bf16[4608,128]{1,0:T(8,128)(2,1)S(1)}, bf16[4608,128]{1,0:T(8,128)(2,1)S(1)}, u32[]{:S(2)}, u32[]{:S(2)}) collective-permute-start(bf16[4608,128]{1,0:T(8,128)(2,1)S(1)} %bitcast.7), channel_id=1, source_target_pairs={{0,1},{1,0},{2,3},{3,2},{4,5},{5,4},{6,7},{7,6},{8,9},{9,8},{10,11... | collective-permute-start | bytes 3538952 | tf_op jit(solution)/shard_map/ppermute | solution.py:381
  47.4 13.5 %copy-start = (bf16[2,128,1024]{2,1,0:T(8,128)(2,1)S(1)}, bf16[2,128,1024]{2,1,0:T(8,128)(2,1)}, u32[]{:S(2)}) copy-start(bf16[2,128,1024]{2,1,0:T(8,128)(2,1)} %constant.26.clone.inv_ref) | copy-start | bytes 1572868
  47.4 13.5 %copy-start.3 = (s32[288,64]{0,1:T(8,128)S(1)}, s32[288,64]{0,1:T(8,128)}, u32[]{:S(2)}) copy-start(s32[288,64]{0,1:T(8,128)} %param.13) | copy-start | bytes 221188
  47.4 13.4 %copy-start.4 = (bf16[8,128,256]{2,1,0:T(8,128)(2,1)S(1)}, bf16[8,128,256]{2,1,0:T(8,128)(2,1)}, u32[]{:S(2)}) copy-start(bf16[8,128,256]{2,1,0:T(8,128)(2,1)} %constant.29.clone.back_ref) | copy-start | bytes 1572868
  47.4 13.4 %copy-start.5 = (bf16[256,512]{1,0:T(8,128)(2,1)S(1)}, bf16[256,512]{1,0:T(8,128)(2,1)}, u32[]{:S(2)}) copy-start(bf16[256,512]{1,0:T(8,128)(2,1)} %constant.27.clone.spread_ref) | copy-start | bytes 786436
  47.4 13.4 %copy-start.6 = (bf16[1024,128]{1,0:T(8,128)(2,1)S(1)}, bf16[1024,128]{1,0:T(8,128)(2,1)}, u32[]{:S(2)}) copy-start(bf16[1024,128]{1,0:T(8,128)(2,1)} %constant.28.clone.fwd_ref) | copy-start | bytes 786436
  76.5 2.8 %collective-permute-start.2 = (bf16[8,4,72,128]{3,2,1,0:T(8,128)(2,1)S(1)}, bf16[8,4,72,128]{3,2,1,0:T(8,128)(2,1)S(1)}, u32[]{:S(2)}, u32[]{:S(2)}) collective-permute-start(bf16[8,4,72,128]{3,2,1,0:T(8,128)(2,1)S(1)} %get-tuple-element.18), channel_id=1, source_target_pairs={{0,1},{1,0},{2,3},{3,2},{4,5},{5,4},{6,7},{7,6},{8,9},{9,8},{10,11... | collective-permute-start | bytes 1769480 | tf_op jit(solution)/shard_map/ppermute | solution.py:390
  78.7 28.2 %copy-start.1 = (bf16[256,512]{1,0:T(8,128)(2,1)S(1)}, bf16[256,512]{1,0:T(8,128)(2,1)}, u32[]{:S(2)}) copy-start(bf16[256,512]{1,0:T(8,128)(2,1)} %constant.30.clone.spread_ref) | copy-start | bytes 786436
  78.7 28.2 %copy-start.2 = (s32[8,288]{1,0:T(8,128)S(1)}, s32[8,288]{1,0:T(8,128)}, u32[]{:S(2)}) copy-start(s32[8,288]{1,0:T(8,128)} %cut_ref.1) | copy-start | bytes 27652
  78.7 2.2 %collective-permute-start.1 = (bf16[8,4,72,128]{3,2,1,0:T(8,128)(2,1)S(1)}, bf16[8,4,72,128]{3,2,1,0:T(8,128)(2,1)S(1)}, u32[]{:S(2)}, u32[]{:S(2)}) collective-permute-start(bf16[8,4,72,128]{3,2,1,0:T(8,128)(2,1)S(1)} %get-tuple-element.16), channel_id=1, source_target_pairs={{0,1},{1,0},{2,3},{3,2},{4,5},{5,4},{6,7},{7,6},{8,9},{9,8},{10,11... | collective-permute-start | bytes 1769480 | tf_op jit(solution)/shard_map/ppermute | solution.py:388

commit v3 on v2

--- a/solution.py
+++ b/solution.py
@@ -62,6 +62,27 @@
     return inv, spread, fwd, back, mixed
 
 
+def repeat_kernel(in_ref, out_ref, sem):
+    copies = [
+        pltpu.make_async_copy(in_ref, out_ref.at[k], sem.at[k]) for k in range(out_ref.shape[0])
+    ]
+    for copy in copies:
+        copy.start()
+    for copy in copies:
+        copy.wait()
+
+
+def repeat(array, times):
+    return pl.pallas_call(
+        repeat_kernel,
+        in_specs=[pl.BlockSpec(memory_space=pltpu.VMEM)],
+        out_specs=pl.BlockSpec(memory_space=pltpu.HBM),
+        scratch_shapes=[pltpu.SemaphoreType.DMA((times,))],
+        out_shape=jax.ShapeDtypeStruct((times,) + array.shape, array.dtype),
+        name="repeat",
+    )(array)
+
+
 def decode_kernel(refl_ref, scale_ref, out_ref):
     blocks = scale_ref.shape[-1]
     for b in range(blocks):
@@ -73,7 +94,7 @@
 
 def decode(refl, scale):
     _, freqs, rows, cols = refl.shape
-    step = 48
+    step = rows
     return pl.pallas_call(
         decode_kernel,
         grid=(freqs, rows // step),
@@ -375,7 +396,7 @@
     group = lax.axis_index(FREQ).astype(jnp.int32)[None]
     inv, spread, fwd, back, mixed = (jnp.asarray(a) for a in constants(8 * freqs, 8))
 
-    shares = jnp.broadcast_to(focus[None], (8, 2, rows, 128)).reshape(16, rows, 128)
+    shares = repeat(focus, 8).reshape(16, rows, 128)
     own = lax.all_to_all(shares, ROWS, 0, 0, tiled=True).reshape(16 * rows, 128)
     decoded = pltpu.with_memory_space_constraint(decode(refl, refl_scale), pltpu.HBM)
     other = lax.ppermute(own, "c", SWAP)

time: 112 us -> 108 us (0.964)
  Pallas kernels: 33.2 us -> 29.5 us
    pallas_call x1, Pallas kernels: 13.8 us -> 8.12 us  [decode(): pl.pallas_call(decode_kernel, grid=(freqs, rows // step), in_specs=[pl.Bl...]
    pallas_call x0 -> x1, Pallas kernels: none -> 1.98 us  [repeat(): pl.pallas_call(repeat_kernel, in_specs=[pl.BlockSpec(memory_space=pltpu.V...]
  transfers between devices with their start and end apart: 3 -> 3, of which waited for: 1 -> 1; matrix products, arithmetic and copies ran while one was open for 1% -> 1% of each run, Pallas kernels for 18% -> 14%
where the time goes in v3:
time: 108 us; the launch traced here: 107 us
  blocking collectives  73.7 us (68%)
  Pallas kernels  29.5 us (27%)
  waiting for transfers between devices  1.63 us (2%)
  local copies, waits for them, and re-layouts  1.09 us (1%)
    all_to_all x1, blocking collectives, on_device(): own = lax.all_to_all(shares, ROWS, 0, 0, tiled=True).reshape(16 * rows, 128)  26.9 us
    all_to_all x1, blocking collectives, on_device(): lax.all_to_all(summed.reshape(64, -1, 128), FREQ + ('zh', 'x'), 0, 0, til...  25.7 us
    all_to_all x1, blocking collectives, on_device(): samples = lax.all_to_all(focused, FREQ, 0, 0, tiled=True)  11.7 us
    all_to_all x1, blocking collectives, on_device(): returned = lax.all_to_all(spectra, FREQ, 0, 0, tiled=True)  9.41 us
    pallas_call x1, Pallas kernels, decode(): pl.pallas_call(decode_kernel, grid=(freqs, rows // step), in_specs=[pl.Bl...  8.12 us
    pallas_call x1, Pallas kernels, first_own(): pl.pallas_call(first_own_kernel, in_specs=[SMEM, SMEM, pl.BlockSpec(memor...  4.62 us
    pallas_call x1, Pallas kernels, final(): pl.pallas_call(final_kernel, in_specs=[VMEM] * 4, out_specs=pl.BlockSpec(...  4.53 us
    pallas_call x1, Pallas kernels, mute(): pl.pallas_call(mute_kernel, in_specs=[SMEM] + [VMEM] * 6, out_specs=VMEM,...  4.15 us
  transfers between devices with their start and end apart: 3, of which 1 were waited for; matrix products, arithmetic and copies ran while one was open for 1% of the time, Pallas kernels for 14%

profile of v3, /device:TPU:0, one launch (start us, length us, event | category | flops | bytes accessed | tf_op | source)
XLA Modules:
  0.0 107.2 jit_solution(7933534006877219620)
XLA Ops:
  0.0 2.0 %repeat.1 = bf16[8,2,288,128]{3,2,1,0:T(8,128)(2,1)} custom-call(bf16[2,288,128]{2,1,0:T(8,128)(2,1)} %in_ref.1), custom_call_target="tpu_custom_call" | custom-call | tf_op jit(solution)/shard_map/repeat/pallas_call | solution.py:76
  2.0 26.9 %all_to_all.20 = bf16[16,288,128]{2,1,0:T(8,128)(2,1)S(1)} all-to-all(bf16[16,288,128]{2,1,0:T(8,128)(2,1)} %bitcast.12), channel_id=1, replica_groups=mesh['y'=4,'zl'=2,'zh'=2,'x'=4,'c'=2] {'zh','x','c'}, dimensions={0} | all-to-all | bytes 2359296 | tf_op jit(solution)/shard_map/all_to_all | solution.py:400
  28.9 0.1 collective-permute-start
  29.0 1.0 copy.11.scale_ref
  30.1 8.1 %decode.1.dec_ref = bf16[2,2,288,4608]{3,2,1,0:T(8,128)(2,1)} custom-call(bf16[2,2,288,4608]{3,2,1,0:T(8,128)(2,1)} %refl_ref.1, f32[2,288,36]{2,1,0:T(8,128)S(1)} %copy.11.scale_ref), custom_call_target="tpu_custom_call" | custom-call | flops 5308416 | bytes 21233664 | tf_op jit(solution)/shard_map/decode/pallas_call | solution.py:98
  38.2 4.6 %first_own.1 = (bf16[8,2,16,288]{3,2,1,0:T(8,128)(2,1)S(1)}, bf16[2,288,4608]{2,1,0:T(8,128)(2,1)S(1)}, bf16[2,288,4608]{2,1,0:T(8,128)(2,1)S(1)}) custom-call(s32[1]{0:T(128)} %bitcast.core_ref, s32[1]{0:T(128)} %bitcast.1.group_ref, bf16[2,2,288,4608]{3,2,1,0:T(8,128)(2,1)} %decode.1.dec_ref, bf16[4608,128]{1,0:T(8,128)(2,1)S(1)} %bitcast.8), custom_call_target="tpu_custom_call" | custom-call | flops 679477248 | bytes 10616832 | tf_op jit(solution)/shard_map/first_own/pallas_call | solution.py:183
  42.8 0.0 copy-start
  42.8 0.0 copy-start.3
  42.9 0.0 copy-start.4
  42.9 0.0 copy-start.5
  42.9 0.0 copy-start.6
  42.9 0.0 collective-permute-done.focus_ref
  42.9 1.7 %first_other.1 = bf16[8,2,16,288]{3,2,1,0:T(8,128)(2,1)S(1)} custom-call(s32[1]{0:T(128)} %bitcast.core_ref, bf16[2,288,4608]{2,1,0:T(8,128)(2,1)S(1)} %get-tuple-element.12.dec_ref.other_ref, bf16[4608,128]{1,0:T(8,128)(2,1)S(1)} %collective-permute-done.focus_ref, bf16[8,2,16,288]{3,2,1,0:T(8,128)(2,1)S(1)} %get-tuple-element.13.half_ref), custom_call_target="tpu_custom_call" | custom-call | flops 679477248 | bytes 5308416 | tf_op jit(solution)/shard_map/first_other/pallas_call | solution.py:202
  44.6 11.7 %all_to_all.21.in_ref = bf16[8,2,16,288]{3,2,1,0:T(8,128)(2,1)S(1)} all-to-all(bf16[8,2,16,288]{3,2,1,0:T(8,128)(2,1)S(1)} %first_other.1), channel_id=1, replica_groups=mesh['y'=4,'zl'=2,'zh'=2,'x'=4,'c'=2] {'y','zl'}, dimensions={0} | all-to-all | bytes 294912 | tf_op jit(solution)/shard_map/all_to_all | solution.py:405
  56.3 0.0 copy-done
  56.3 0.0 copy-done.3
  56.3 0.0 copy-done.4
  56.3 0.0 copy-done.5
  56.3 0.0 copy-done.6
  56.3 4.2 %mute.1 = bf16[8,2,16,288]{3,2,1,0:T(8,128)(2,1)S(1)} custom-call(s32[1]{0:T(128)} %bitcast.1.group_ref, bf16[8,2,16,288]{3,2,1,0:T(8,128)(2,1)S(1)} %all_to_all.21.in_ref, s32[64,288]{1,0:T(8,128)S(1)} %bitcast.11, bf16[256,512]{1,0:T(8,128)(2,1)S(1)} %copy-done.5, bf16[2,128,1024]{2,1,0:T(8,128)(2,1)S(1)} %copy-done, bf16[1024,128]{1,0:T(8,128)(2,1)S(1)} %copy-done.6, ...), custom_call_target="tpu_custom_call" | custom-call | flops 1207959552 | bytes 4194304 | tf_op jit(solution)/shard_map/mute/pallas_call | solution.py:238
  60.5 9.4 %all_to_all.22.ret_ref = bf16[8,2,16,288]{3,2,1,0:T(8,128)(2,1)S(1)} all-to-all(bf16[8,2,16,288]{3,2,1,0:T(8,128)(2,1)S(1)} %mute.1), channel_id=1, replica_groups=mesh['y'=4,'zl'=2,'zh'=2,'x'=4,'c'=2] {'y','zl'}, dimensions={0} | all-to-all | bytes 294912 | tf_op jit(solution)/shard_map/all_to_all | solution.py:407
  69.9 2.0 %second_product.3 = (bf16[8,4,72,128]{3,2,1,0:T(8,128)(2,1)S(1)}, bf16[8,4,72,128]{3,2,1,0:T(8,128)(2,1)S(1)}) custom-call(s32[1]{0:T(128)} %bitcast.core_ref, bf16[8,2,16,288]{3,2,1,0:T(8,128)(2,1)S(1)} %all_to_all.22.ret_ref, bf16[2,288,4608]{2,1,0:T(8,128)(2,1)S(1)} %get-tuple-element.14.own_ref, bf16[2,288,4608]{2,1,0:T(8,128)(2,1)S(1)} %get-tuple-element.12.dec_ref.other_ref), custom_call_target="tpu_custom_call" | custom-call | flops 679477248 | bytes 6635520 | tf_op jit(solution)/shard_map/second_product/pallas_call | solution.py:305
  71.9 0.1 collective-permute-start.2
  72.0 2.1 %second_product.2 = (bf16[8,4,72,128]{3,2,1,0:T(8,128)(2,1)S(1)}, bf16[8,4,72,128]{3,2,1,0:T(8,128)(2,1)S(1)}) custom-call(s32[1]{0:T(128)} %bitcast.core_ref, bf16[8,2,16,288]{3,2,1,0:T(8,128)(2,1)S(1)} %all_to_all.22.ret_ref, bf16[2,288,4608]{2,1,0:T(8,128)(2,1)S(1)} %get-tuple-element.14.own_ref, bf16[2,288,4608]{2,1,0:T(8,128)(2,1)S(1)} %get-tuple-element.12.dec_ref.other_ref), custom_call_target="tpu_custom_call" | custom-call | flops 679477248 | bytes 6635520 | tf_op jit(solution)/shard_map/second_product/pallas_call | solution.py:305
  74.1 0.0 copy-start.1
  74.1 0.0 copy-start.2
  74.2 0.7 collective-permute-start.1
  74.9 0.0 collective-permute-done.2.d_ref
  74.9 1.6 %collective-permute-done.1.b_ref = bf16[8,4,72,128]{3,2,1,0:T(8,128)(2,1)S(1)} collective-permute-done((bf16[8,4,72,128]{3,2,1,0:T(8,128)(2,1)S(1)}, bf16[8,4,72,128]{3,2,1,0:T(8,128)(2,1)S(1)}, u32[]{:S(2)}, u32[]{:S(2)}) %collective-permute-start.1) | collective-permute-done | bytes 589856 | tf_op jit(solution)/shard_map/ppermute | solution.py:409
  76.5 0.3 merge.1
  76.8 25.7 %all_to_all.23 = bf16[64,72,128]{2,1,0:T(8,128)(2,1)S(1)} all-to-all(bf16[64,72,128]{2,1,0:T(8,128)(2,1)S(1)} %bitcast.10), channel_id=1, replica_groups=mesh['y'=4,'zl'=2,'zh'=2,'x'=4,'c'=2] {'y','zl','zh','x'}, dimensions={0} | all-to-all | bytes 2359296 | tf_op jit(solution)/shard_map/all_to_all | solution.py:413
  102.5 0.0 copy-done.1
  102.5 0.0 copy-done.2
  102.5 4.5 %final.1 = f32[8,288,1024]{2,1,0:T(8,128)} custom-call(bf16[8,8,72,128]{3,2,1,0:T(8,128)(2,1)S(1)} %bitcast.9, s32[8,288]{1,0:T(8,128)S(1)} %copy-done.2, bf16[256,512]{1,0:T(8,128)(2,1)S(1)} %copy-done.1, bf16[2,128,1024]{2,1,0:T(8,128)(2,1)S(1)} %copy-done), custom_call_target="tpu_custom_call" | custom-call | flops 603979776 | bytes 12582912 | tf_op jit(solution)/shard_map/final/pallas_call | solution.py:375
Async XLA Ops:
  28.9 14.0 %collective-permute-start = (bf16[4608,128]{1,0:T(8,128)(2,1)S(1)}, bf16[4608,128]{1,0:T(8,128)(2,1)S(1)}, u32[]{:S(2)}, u32[]{:S(2)}) collective-permute-start(bf16[4608,128]{1,0:T(8,128)(2,1)S(1)} %bitcast.7), channel_id=1, source_target_pairs={{0,1},{1,0},{2,3},{3,2},{4,5},{5,4},{6,7},{7,6},{8,9},{9,8},{10,11... | collective-permute-start | bytes 3538952 | tf_op jit(solution)/shard_map/ppermute | solution.py:402
  42.8 13.5 %copy-start = (bf16[2,128,1024]{2,1,0:T(8,128)(2,1)S(1)}, bf16[2,128,1024]{2,1,0:T(8,128)(2,1)}, u32[]{:S(2)}) copy-start(bf16[2,128,1024]{2,1,0:T(8,128)(2,1)} %constant.26.clone.inv_ref) | copy-start | bytes 1572868
  42.8 13.5 %copy-start.3 = (s32[288,64]{0,1:T(8,128)S(1)}, s32[288,64]{0,1:T(8,128)}, u32[]{:S(2)}) copy-start(s32[288,64]{0,1:T(8,128)} %param.13) | copy-start | bytes 221188
  42.9 13.4 %copy-start.4 = (bf16[8,128,256]{2,1,0:T(8,128)(2,1)S(1)}, bf16[8,128,256]{2,1,0:T(8,128)(2,1)}, u32[]{:S(2)}) copy-start(bf16[8,128,256]{2,1,0:T(8,128)(2,1)} %constant.29.clone.back_ref) | copy-start | bytes 1572868
  42.9 13.4 %copy-start.5 = (bf16[256,512]{1,0:T(8,128)(2,1)S(1)}, bf16[256,512]{1,0:T(8,128)(2,1)}, u32[]{:S(2)}) copy-start(bf16[256,512]{1,0:T(8,128)(2,1)} %constant.27.clone.spread_ref) | copy-start | bytes 786436
  42.9 13.4 %copy-start.6 = (bf16[1024,128]{1,0:T(8,128)(2,1)S(1)}, bf16[1024,128]{1,0:T(8,128)(2,1)}, u32[]{:S(2)}) copy-start(bf16[1024,128]{1,0:T(8,128)(2,1)} %constant.28.clone.fwd_ref) | copy-start | bytes 786436
  71.9 3.0 %collective-permute-start.2 = (bf16[8,4,72,128]{3,2,1,0:T(8,128)(2,1)S(1)}, bf16[8,4,72,128]{3,2,1,0:T(8,128)(2,1)S(1)}, u32[]{:S(2)}, u32[]{:S(2)}) collective-permute-start(bf16[8,4,72,128]{3,2,1,0:T(8,128)(2,1)S(1)} %get-tuple-element.18), channel_id=1, source_target_pairs={{0,1},{1,0},{2,3},{3,2},{4,5},{5,4},{6,7},{7,6},{8,9},{9,8},{10,11... | collective-permute-start | bytes 1769480 | tf_op jit(solution)/shard_map/ppermute | solution.py:411
  74.1 28.3 %copy-start.1 = (bf16[256,512]{1,0:T(8,128)(2,1)S(1)}, bf16[256,512]{1,0:T(8,128)(2,1)}, u32[]{:S(2)}) copy-start(bf16[256,512]{1,0:T(8,128)(2,1)} %constant.30.clone.spread_ref) | copy-start | bytes 786436
  74.1 28.3 %copy-start.2 = (s32[8,288]{1,0:T(8,128)S(1)}, s32[8,288]{1,0:T(8,128)}, u32[]{:S(2)}) copy-start(s32[8,288]{1,0:T(8,128)} %cut_ref.1) | copy-start | bytes 27652
  74.2 2.4 %collective-permute-start.1 = (bf16[8,4,72,128]{3,2,1,0:T(8,128)(2,1)S(1)}, bf16[8,4,72,128]{3,2,1,0:T(8,128)(2,1)S(1)}, u32[]{:S(2)}, u32[]{:S(2)}) collective-permute-start(bf16[8,4,72,128]{3,2,1,0:T(8,128)(2,1)S(1)} %get-tuple-element.16), channel_id=1, source_target_pairs={{0,1},{1,0},{2,3},{3,2},{4,5},{5,4},{6,7},{7,6},{8,9},{9,8},{10,11... | collective-permute-start | bytes 1769480 | tf_op jit(solution)/shard_map/ppermute | solution.py:409

commit v4 on v3

--- a/solution.py
+++ b/solution.py
@@ -343,6 +343,7 @@
 
 def final_kernel(in_ref, cut_ref, spread_ref, inv_ref, out_ref, wide_ref, slab_ref, sem):
     per = in_ref.shape[2] // 8
+    rows = cut_ref.shape[1]
     total = in_ref[:, 0].astype(F32)
     for j in range(1, 8):
         total += in_ref[:, j].astype(F32)
@@ -356,17 +357,28 @@
         wide_ref[q] = wide[:, q * 128 : (q + 1) * 128].astype(BF)
     edge = cut_ref[...].astype(F32).T
 
+    third = rows // 3
+
     def out(p):
-        return pltpu.make_async_copy(slab_ref.at[p], out_ref.at[p], sem.at[p])
+        return [
+            pltpu.make_async_copy(
+                slab_ref.at[p, h * third : (h + 1) * third],
+                out_ref.at[p, h * third : (h + 1) * third],
+                sem.at[p, h],
+            )
+            for h in range(3)
+        ]
 
     for p in range(8):
         traces = jnp.dot(wide_ref[p // 2], inv_ref[p % 2], preferred_element_type=F32)
         cut = edge[:, p : p + 1].astype(jnp.int32)
         time = lax.broadcasted_iota(jnp.int32, traces.shape, 1)
         slab_ref[p] = jnp.where(time < cut, traces, 0.0)
-        out(p).start()
+        for copy in out(p):
+            copy.start()
     for p in range(8):
-        out(p).wait()
+        for copy in out(p):
+            copy.wait()
 
 
 def final(partials, cut, spread, inv):
@@ -379,7 +391,7 @@
         scratch_shapes=[
             pltpu.VMEM((4, rows, 128), BF),
             pltpu.VMEM((8, rows, NT), F32),
-            pltpu.SemaphoreType.DMA((8,)),
+            pltpu.SemaphoreType.DMA((8, 3)),
         ],
         out_shape=jax.ShapeDtypeStruct((8, rows, NT), F32),
         compiler_params=pltpu.CompilerParams(vmem_limit_bytes=24 * MB),

time: 108 us -> 108 us (level)
  no operation moved by 1% of the time
where the time goes in v4:
time: 108 us; the launch traced here: 107 us
  blocking collectives  73.7 us (68%)
  Pallas kernels  29.6 us (27%)
  waiting for transfers between devices  1.63 us (2%)
  local copies, waits for them, and re-layouts  1.09 us (1%)
    all_to_all x1, blocking collectives, on_device(): own = lax.all_to_all(shares, ROWS, 0, 0, tiled=True).reshape(16 * rows, 128)  26.9 us
    all_to_all x1, blocking collectives, on_device(): lax.all_to_all(summed.reshape(64, -1, 128), FREQ + ('zh', 'x'), 0, 0, til...  25.7 us
    all_to_all x1, blocking collectives, on_device(): samples = lax.all_to_all(focused, FREQ, 0, 0, tiled=True)  11.7 us
    all_to_all x1, blocking collectives, on_device(): returned = lax.all_to_all(spectra, FREQ, 0, 0, tiled=True)  9.41 us
    pallas_call x1, Pallas kernels, decode(): pl.pallas_call(decode_kernel, grid=(freqs, rows // step), in_specs=[pl.Bl...  8.12 us
    pallas_call x1, Pallas kernels, final(): pl.pallas_call(final_kernel, in_specs=[VMEM] * 4, out_specs=pl.BlockSpec(...  4.63 us
    pallas_call x1, Pallas kernels, first_own(): pl.pallas_call(first_own_kernel, in_specs=[SMEM, SMEM, pl.BlockSpec(memor...  4.62 us
    pallas_call x1, Pallas kernels, mute(): pl.pallas_call(mute_kernel, in_specs=[SMEM] + [VMEM] * 6, out_specs=VMEM,...  4.15 us
  transfers between devices with their start and end apart: 3, of which 1 were waited for; matrix products, arithmetic and copies ran while one was open for 1% of the time, Pallas kernels for 14%

profile of v4, /device:TPU:0, one launch (start us, length us, event | category | flops | bytes accessed | tf_op | source)
XLA Modules:
  0.0 107.3 jit_solution(8766538388982287494)
XLA Ops:
  0.0 2.0 %repeat.1 = bf16[8,2,288,128]{3,2,1,0:T(8,128)(2,1)} custom-call(bf16[2,288,128]{2,1,0:T(8,128)(2,1)} %in_ref.1), custom_call_target="tpu_custom_call" | custom-call | tf_op jit(solution)/shard_map/repeat/pallas_call | solution.py:76
  2.0 26.9 %all_to_all.20 = bf16[16,288,128]{2,1,0:T(8,128)(2,1)S(1)} all-to-all(bf16[16,288,128]{2,1,0:T(8,128)(2,1)} %bitcast.12), channel_id=1, replica_groups=mesh['y'=4,'zl'=2,'zh'=2,'x'=4,'c'=2] {'zh','x','c'}, dimensions={0} | all-to-all | bytes 2359296 | tf_op jit(solution)/shard_map/all_to_all | solution.py:412
  28.9 0.1 collective-permute-start
  29.0 1.0 copy.11.scale_ref
  30.1 8.1 %decode.1.dec_ref = bf16[2,2,288,4608]{3,2,1,0:T(8,128)(2,1)} custom-call(bf16[2,2,288,4608]{3,2,1,0:T(8,128)(2,1)} %refl_ref.1, f32[2,288,36]{2,1,0:T(8,128)S(1)} %copy.11.scale_ref), custom_call_target="tpu_custom_call" | custom-call | flops 5308416 | bytes 21233664 | tf_op jit(solution)/shard_map/decode/pallas_call | solution.py:98
  38.2 4.6 %first_own.1 = (bf16[8,2,16,288]{3,2,1,0:T(8,128)(2,1)S(1)}, bf16[2,288,4608]{2,1,0:T(8,128)(2,1)S(1)}, bf16[2,288,4608]{2,1,0:T(8,128)(2,1)S(1)}) custom-call(s32[1]{0:T(128)} %bitcast.core_ref, s32[1]{0:T(128)} %bitcast.1.group_ref, bf16[2,2,288,4608]{3,2,1,0:T(8,128)(2,1)} %decode.1.dec_ref, bf16[4608,128]{1,0:T(8,128)(2,1)S(1)} %bitcast.8), custom_call_target="tpu_custom_call" | custom-call | flops 679477248 | bytes 10616832 | tf_op jit(solution)/shard_map/first_own/pallas_call | solution.py:183
  42.8 0.0 copy-start
  42.8 0.0 copy-start.3
  42.9 0.0 copy-start.4
  42.9 0.0 copy-start.5
  42.9 0.0 copy-start.6
  42.9 0.0 collective-permute-done.focus_ref
  42.9 1.7 %first_other.1 = bf16[8,2,16,288]{3,2,1,0:T(8,128)(2,1)S(1)} custom-call(s32[1]{0:T(128)} %bitcast.core_ref, bf16[2,288,4608]{2,1,0:T(8,128)(2,1)S(1)} %get-tuple-element.12.dec_ref.other_ref, bf16[4608,128]{1,0:T(8,128)(2,1)S(1)} %collective-permute-done.focus_ref, bf16[8,2,16,288]{3,2,1,0:T(8,128)(2,1)S(1)} %get-tuple-element.13.half_ref), custom_call_target="tpu_custom_call" | custom-call | flops 679477248 | bytes 5308416 | tf_op jit(solution)/shard_map/first_other/pallas_call | solution.py:202
  44.6 11.7 %all_to_all.21.in_ref = bf16[8,2,16,288]{3,2,1,0:T(8,128)(2,1)S(1)} all-to-all(bf16[8,2,16,288]{3,2,1,0:T(8,128)(2,1)S(1)} %first_other.1), channel_id=1, replica_groups=mesh['y'=4,'zl'=2,'zh'=2,'x'=4,'c'=2] {'y','zl'}, dimensions={0} | all-to-all | bytes 294912 | tf_op jit(solution)/shard_map/all_to_all | solution.py:417
  56.3 0.0 copy-done
  56.3 0.0 copy-done.3
  56.3 0.0 copy-done.4
  56.3 0.0 copy-done.5
  56.3 0.0 copy-done.6
  56.3 4.2 %mute.1 = bf16[8,2,16,288]{3,2,1,0:T(8,128)(2,1)S(1)} custom-call(s32[1]{0:T(128)} %bitcast.1.group_ref, bf16[8,2,16,288]{3,2,1,0:T(8,128)(2,1)S(1)} %all_to_all.21.in_ref, s32[64,288]{1,0:T(8,128)S(1)} %bitcast.11, bf16[256,512]{1,0:T(8,128)(2,1)S(1)} %copy-done.5, bf16[2,128,1024]{2,1,0:T(8,128)(2,1)S(1)} %copy-done, bf16[1024,128]{1,0:T(8,128)(2,1)S(1)} %copy-done.6, ...), custom_call_target="tpu_custom_call" | custom-call | flops 1207959552 | bytes 4194304 | tf_op jit(solution)/shard_map/mute/pallas_call | solution.py:238
  60.5 9.4 %all_to_all.22.ret_ref = bf16[8,2,16,288]{3,2,1,0:T(8,128)(2,1)S(1)} all-to-all(bf16[8,2,16,288]{3,2,1,0:T(8,128)(2,1)S(1)} %mute.1), channel_id=1, replica_groups=mesh['y'=4,'zl'=2,'zh'=2,'x'=4,'c'=2] {'y','zl'}, dimensions={0} | all-to-all | bytes 294912 | tf_op jit(solution)/shard_map/all_to_all | solution.py:419
  69.9 2.0 %second_product.3 = (bf16[8,4,72,128]{3,2,1,0:T(8,128)(2,1)S(1)}, bf16[8,4,72,128]{3,2,1,0:T(8,128)(2,1)S(1)}) custom-call(s32[1]{0:T(128)} %bitcast.core_ref, bf16[8,2,16,288]{3,2,1,0:T(8,128)(2,1)S(1)} %all_to_all.22.ret_ref, bf16[2,288,4608]{2,1,0:T(8,128)(2,1)S(1)} %get-tuple-element.14.own_ref, bf16[2,288,4608]{2,1,0:T(8,128)(2,1)S(1)} %get-tuple-element.12.dec_ref.other_ref), custom_call_target="tpu_custom_call" | custom-call | flops 679477248 | bytes 6635520 | tf_op jit(solution)/shard_map/second_product/pallas_call | solution.py:305
  71.9 0.1 collective-permute-start.2
  72.0 2.1 %second_product.2 = (bf16[8,4,72,128]{3,2,1,0:T(8,128)(2,1)S(1)}, bf16[8,4,72,128]{3,2,1,0:T(8,128)(2,1)S(1)}) custom-call(s32[1]{0:T(128)} %bitcast.core_ref, bf16[8,2,16,288]{3,2,1,0:T(8,128)(2,1)S(1)} %all_to_all.22.ret_ref, bf16[2,288,4608]{2,1,0:T(8,128)(2,1)S(1)} %get-tuple-element.14.own_ref, bf16[2,288,4608]{2,1,0:T(8,128)(2,1)S(1)} %get-tuple-element.12.dec_ref.other_ref), custom_call_target="tpu_custom_call" | custom-call | flops 679477248 | bytes 6635520 | tf_op jit(solution)/shard_map/second_product/pallas_call | solution.py:305
  74.1 0.0 copy-start.1
  74.1 0.0 copy-start.2
  74.2 0.7 collective-permute-start.1
  74.9 0.0 collective-permute-done.2.d_ref
  74.9 1.6 %collective-permute-done.1.b_ref = bf16[8,4,72,128]{3,2,1,0:T(8,128)(2,1)S(1)} collective-permute-done((bf16[8,4,72,128]{3,2,1,0:T(8,128)(2,1)S(1)}, bf16[8,4,72,128]{3,2,1,0:T(8,128)(2,1)S(1)}, u32[]{:S(2)}, u32[]{:S(2)}) %collective-permute-start.1) | collective-permute-done | bytes 589856 | tf_op jit(solution)/shard_map/ppermute | solution.py:421
  76.5 0.3 merge.1
  76.8 25.7 %all_to_all.23 = bf16[64,72,128]{2,1,0:T(8,128)(2,1)S(1)} all-to-all(bf16[64,72,128]{2,1,0:T(8,128)(2,1)S(1)} %bitcast.10), channel_id=1, replica_groups=mesh['y'=4,'zl'=2,'zh'=2,'x'=4,'c'=2] {'y','zl','zh','x'}, dimensions={0} | all-to-all | bytes 2359296 | tf_op jit(solution)/shard_map/all_to_all | solution.py:425
  102.5 0.0 copy-done.1
  102.5 0.0 copy-done.2
  102.5 4.6 %final.1 = f32[8,288,1024]{2,1,0:T(8,128)} custom-call(bf16[8,8,72,128]{3,2,1,0:T(8,128)(2,1)S(1)} %bitcast.9, s32[8,288]{1,0:T(8,128)S(1)} %copy-done.2, bf16[256,512]{1,0:T(8,128)(2,1)S(1)} %copy-done.1, bf16[2,128,1024]{2,1,0:T(8,128)(2,1)S(1)} %copy-done), custom_call_target="tpu_custom_call" | custom-call | flops 603979776 | bytes 12582912 | tf_op jit(solution)/shard_map/final/pallas_call | solution.py:387
Async XLA Ops:
  28.9 14.0 %collective-permute-start = (bf16[4608,128]{1,0:T(8,128)(2,1)S(1)}, bf16[4608,128]{1,0:T(8,128)(2,1)S(1)}, u32[]{:S(2)}, u32[]{:S(2)}) collective-permute-start(bf16[4608,128]{1,0:T(8,128)(2,1)S(1)} %bitcast.7), channel_id=1, source_target_pairs={{0,1},{1,0},{2,3},{3,2},{4,5},{5,4},{6,7},{7,6},{8,9},{9,8},{10,11... | collective-permute-start | bytes 3538952 | tf_op jit(solution)/shard_map/ppermute | solution.py:414
  42.8 13.5 %copy-start = (bf16[2,128,1024]{2,1,0:T(8,128)(2,1)S(1)}, bf16[2,128,1024]{2,1,0:T(8,128)(2,1)}, u32[]{:S(2)}) copy-start(bf16[2,128,1024]{2,1,0:T(8,128)(2,1)} %constant.26.clone.inv_ref) | copy-start | bytes 1572868
  42.8 13.5 %copy-start.3 = (s32[288,64]{0,1:T(8,128)S(1)}, s32[288,64]{0,1:T(8,128)}, u32[]{:S(2)}) copy-start(s32[288,64]{0,1:T(8,128)} %param.13) | copy-start | bytes 221188
  42.9 13.4 %copy-start.4 = (bf16[8,128,256]{2,1,0:T(8,128)(2,1)S(1)}, bf16[8,128,256]{2,1,0:T(8,128)(2,1)}, u32[]{:S(2)}) copy-start(bf16[8,128,256]{2,1,0:T(8,128)(2,1)} %constant.29.clone.back_ref) | copy-start | bytes 1572868
  42.9 13.4 %copy-start.5 = (bf16[256,512]{1,0:T(8,128)(2,1)S(1)}, bf16[256,512]{1,0:T(8,128)(2,1)}, u32[]{:S(2)}) copy-start(bf16[256,512]{1,0:T(8,128)(2,1)} %constant.27.clone.spread_ref) | copy-start | bytes 786436
  42.9 13.4 %copy-start.6 = (bf16[1024,128]{1,0:T(8,128)(2,1)S(1)}, bf16[1024,128]{1,0:T(8,128)(2,1)}, u32[]{:S(2)}) copy-start(bf16[1024,128]{1,0:T(8,128)(2,1)} %constant.28.clone.fwd_ref) | copy-start | bytes 786436
  71.9 3.0 %collective-permute-start.2 = (bf16[8,4,72,128]{3,2,1,0:T(8,128)(2,1)S(1)}, bf16[8,4,72,128]{3,2,1,0:T(8,128)(2,1)S(1)}, u32[]{:S(2)}, u32[]{:S(2)}) collective-permute-start(bf16[8,4,72,128]{3,2,1,0:T(8,128)(2,1)S(1)} %get-tuple-element.18), channel_id=1, source_target_pairs={{0,1},{1,0},{2,3},{3,2},{4,5},{5,4},{6,7},{7,6},{8,9},{9,8},{10,11... | collective-permute-start | bytes 1769480 | tf_op jit(solution)/shard_map/ppermute | solution.py:423
  74.1 28.3 %copy-start.1 = (bf16[256,512]{1,0:T(8,128)(2,1)S(1)}, bf16[256,512]{1,0:T(8,128)(2,1)}, u32[]{:S(2)}) copy-start(bf16[256,512]{1,0:T(8,128)(2,1)} %constant.30.clone.spread_ref) | copy-start | bytes 786436
  74.1 28.3 %copy-start.2 = (s32[8,288]{1,0:T(8,128)S(1)}, s32[8,288]{1,0:T(8,128)}, u32[]{:S(2)}) copy-start(s32[8,288]{1,0:T(8,128)} %cut_ref.1) | copy-start | bytes 27652
  74.2 2.4 %collective-permute-start.1 = (bf16[8,4,72,128]{3,2,1,0:T(8,128)(2,1)S(1)}, bf16[8,4,72,128]{3,2,1,0:T(8,128)(2,1)S(1)}, u32[]{:S(2)}, u32[]{:S(2)}) collective-permute-start(bf16[8,4,72,128]{3,2,1,0:T(8,128)(2,1)S(1)} %get-tuple-element.16), channel_id=1, source_target_pairs={{0,1},{1,0},{2,3},{3,2},{4,5},{5,4},{6,7},{7,6},{8,9},{9,8},{10,11... | collective-permute-start | bytes 1769480 | tf_op jit(solution)/shard_map/ppermute | solution.py:421
